TPU v7x, 256 devices: a whole 4x4x8 slice. The times are simulated.
256 devices in a mesh: group: 8 (over z), date: 32 (over x, y, core).
Axes of the slice: x: 4, y: 4, z: 8, core: 2. Of those that a mesh axis runs over, the one named last changes fastest.
Arguments:
- pixels: bfloat16 [13, 24, 512, 4096], P(None, None, 'date', 'group'), may hold values from -6 to 6
- counts: int32 [512, 4096], P('date', 'group'), may hold values from 1 to 24
- edge_pixels: bfloat16 [13, 8, 512, 512], P(None, None, 'date', 'group'), may hold values from 1.5 to 6
- edge_mask: int32 [8, 512, 512], P(None, 'date', 'group'), may hold values 0 or 1
- straddle_lot: int32 [512], P('group'), may hold values from 0 to 511, as said below
- date_days: int32 [512], replicated, may hold values from 0 to 1022, as said below
- w_first: bfloat16 [32, 13], replicated, may hold values from -1.75 to 1.75
- b_first: float32 [32], replicated, may hold values from -3 to 3
- w_second: bfloat16 [128, 32], replicated, may hold values from -1 to 1
- b_second: float32 [128], replicated, may hold values from -3 to 3
- w_pool: bfloat16 [256, 128], replicated, may hold values from -0.375 to 0.375
- b_pool: float32 [128], replicated, may hold values from -3 to 3
- ln_one: float32 [128], replicated, may hold values from 0.5 to 1.5
- w_query: bfloat16 [128, 128], replicated
- w_key: bfloat16 [128, 128], replicated
- w_value: bfloat16 [128, 128], replicated, may hold values from -0.5 to 0.5
- w_out: bfloat16 [128, 128], replicated, may hold values from -0.5 to 0.5
- ln_two: float32 [128], replicated, may hold values from 0.5 to 1.5
- w_up: bfloat16 [128, 512], replicated, may hold values from -0.5 to 0.5
- w_down: bfloat16 [512, 128], replicated, may hold values from -0.25 to 0.25
Outputs:
- encoded: bfloat16 [512, 4096, 128], P(None, ('group', 'date'))
Inputs may be any that keep to these rules, and one draw needn't show every extreme that they name: `straddle_lot`: within each lot group's 64 entries the lots are distinct. `date_days`: strictly increasing day numbers; the first is 0 and the last is 1022.
All inputs are finite; a program needn't handle non-finite values. No bound on the sum of `edge_mask` on one device may be relied on, other than what follows from the above.
Results may differ from a plain program's by a relative error of at most 0.012.
The roundings to bfloat16 on the way count: a program that leaves them out, or rounds other values in their place, can miss the bound.
Values may be sent and summed in bfloat16 or wider, within the bound.
No kernel may reach another device: no remote copies, remote signals or barrier semaphores. Data moves between devices by JAX's collectives and lax.ppermute only.
A program may use at most 128 MiB of HBM per device.

v0:
```python
import math

import jax
import jax.numpy as jnp
from jax import lax
from jax.sharding import PartitionSpec as P

HEADS = 4


VAR_FLOOR = 0.05
NORM_EPS = 1e-05


def passed_along(block, axis, distance):
    devices = range(lax.axis_size(axis))
    route = [((i - distance) % len(devices), i) for i in devices]
    return lax.ppermute(block, axis, route)


def pixel_stats(patch, usable, w_first, b_first, w_second, b_second):
    band_count, slot_count, columns = patch.shape
    flattened = patch.reshape(band_count, slot_count * columns)
    h_one = jnp.maximum(
        jnp.dot(w_first, flattened, preferred_element_type=jnp.float32) + b_first[:, None], 0.0
    ).astype(jnp.bfloat16)
    h_two = jnp.maximum(
        jnp.dot(w_second, h_one, preferred_element_type=jnp.float32) + b_second[:, None], 0.0
    )
    h_two = h_two.reshape(h_two.shape[0], slot_count, columns)
    weighted = h_two * usable[None]
    return (jnp.sum(weighted, axis=1), jnp.sum(weighted * h_two, axis=1), jnp.sum(usable, axis=0))


def pool_stats(sum_all, square_all, count_all):
    average = sum_all / count_all
    spread = jnp.sqrt(jnp.maximum(square_all / count_all - average * average, VAR_FLOOR))
    return jnp.concatenate([average, spread], axis=-2).astype(jnp.bfloat16)


def position_code(day_numbers, model_width):
    half_ids = jnp.arange(model_width // 2, dtype=jnp.float32)
    freq_rate = jnp.exp(-(2.0 * half_ids / model_width) * math.log(1000.0))
    phase_angle = day_numbers.astype(jnp.float32)[:, None] * freq_rate[None]
    return jnp.stack([jnp.sin(phase_angle), jnp.cos(phase_angle)], axis=-1).reshape(
        day_numbers.shape[0], model_width
    )


def layer_norm(inputs, scale_gain):
    average = jnp.mean(inputs, axis=-1, keepdims=True)
    centered = inputs - average
    variance = jnp.mean(centered * centered, axis=-1, keepdims=True)
    return centered * lax.rsqrt(variance + NORM_EPS) * scale_gain


def temporal_layer(series, params):
    ln_one, w_query, w_key, w_value, w_out, ln_two, w_up, w_down = params
    length, model_width = series.shape
    head_width = model_width // HEADS
    carried = series.astype(jnp.float32)
    normed = layer_norm(carried, ln_one).astype(jnp.bfloat16)
    queries = (
        jnp.dot(normed, w_query, preferred_element_type=jnp.float32)
        .astype(jnp.bfloat16)
        .reshape(length, HEADS, head_width)
    )
    key_rows = (
        jnp.dot(normed, w_key, preferred_element_type=jnp.float32)
        .astype(jnp.bfloat16)
        .reshape(length, HEADS, head_width)
    )
    values = (
        jnp.dot(normed, w_value, preferred_element_type=jnp.float32)
        .astype(jnp.bfloat16)
        .reshape(length, HEADS, head_width)
    )
    scores = jnp.einsum(
        "qhd,khd->hqk", queries, key_rows, preferred_element_type=jnp.float32
    ) / math.sqrt(head_width)
    att_weights = jax.nn.softmax(scores, axis=-1).astype(jnp.bfloat16)
    mixture = jnp.einsum("hqk,khd->qhd", att_weights, values, preferred_element_type=jnp.float32)
    mixture = mixture.reshape(length, model_width).astype(jnp.bfloat16)
    carried = carried + jnp.dot(mixture, w_out, preferred_element_type=jnp.float32)
    normed_two = layer_norm(carried, ln_two).astype(jnp.bfloat16)
    hidden = jax.nn.gelu(
        jnp.dot(normed_two, w_up, preferred_element_type=jnp.float32), approximate=False
    ).astype(jnp.bfloat16)
    return (carried + jnp.dot(hidden, w_down, preferred_element_type=jnp.float32)).astype(
        jnp.bfloat16
    )


def attend_lots(embedded, params):
    series_all = jnp.moveaxis(embedded[:, 0], 1, 0)
    encoded = lax.map(lambda series: temporal_layer(series, params), series_all)
    return jnp.moveaxis(encoded, 0, 1)[:, None]


def per_device(
    pixels,
    counts,
    edge_pixels,
    edge_mask,
    straddle_lot,
    date_days,
    w_first,
    b_first,
    w_second,
    b_second,
    w_pool,
    b_pool,
    ln_one,
    w_query,
    w_key,
    w_value,
    w_out,
    ln_two,
    w_up,
    w_down,
):
    band_count, slot_total, date_dev, lots_g = pixels.shape
    edge_slots = edge_pixels.shape[1]
    str_g = edge_pixels.shape[3]
    peer_count = lax.axis_size("date")
    lot_dev = lots_g // peer_count
    date_total = date_dev * peer_count
    model_width = w_pool.shape[1]
    day_code = position_code(date_days, model_width)
    slot_ids = jnp.arange(slot_total, dtype=jnp.int32)
    params = (ln_one, w_query, w_key, w_value, w_out, ln_two, w_up, w_down)

    def per_date(inputs):
        patch, filled = inputs
        usable = (slot_ids[:, None] < filled[None, :]).astype(jnp.float32)
        return pixel_stats(patch, usable, w_first, b_first, w_second, b_second)

    sum_all, square_all, count_all = lax.map(per_date, (jnp.moveaxis(pixels, 2, 0), counts))
    flat_patch = edge_pixels.reshape(band_count, edge_slots, date_dev * str_g)
    flat_usable = edge_mask.astype(jnp.float32).reshape(edge_slots, date_dev * str_g)
    edge_sum, edge_square, edge_count = pixel_stats(
        flat_patch, flat_usable, w_first, b_first, w_second, b_second
    )
    edge_sum, edge_square, edge_count = (
        edge_sum.reshape(-1, date_dev, str_g),
        edge_square.reshape(-1, date_dev, str_g),
        edge_count.reshape(date_dev, str_g),
    )
    edge_sum, edge_square, edge_count = passed_along(
        (edge_sum, edge_square, edge_count), "group", 1
    )
    sum_all = sum_all.at[:, :, straddle_lot].add(jnp.swapaxes(edge_sum, 0, 1))
    square_all = square_all.at[:, :, straddle_lot].add(jnp.swapaxes(edge_square, 0, 1))
    count_all = count_all.at[:, straddle_lot].add(edge_count)
    pooled = pool_stats(sum_all, square_all, count_all[:, None, :])
    payload = jnp.swapaxes(pooled, 1, 2).reshape(date_dev, peer_count, lot_dev, pooled.shape[1])
    projected = jnp.einsum(
        "dxic,ce->dxie",
        lax.all_to_all(payload, "date", split_axis=1, concat_axis=0, tiled=True),
        w_pool,
        preferred_element_type=jnp.float32,
    )
    projected = (projected + b_pool + day_code[:, None, None, :]).astype(jnp.bfloat16)
    result = attend_lots(projected, params)
    return result.reshape(date_total, lot_dev, model_width)


def solution(mesh):
    return jax.shard_map(
        per_device,
        mesh=mesh,
        in_specs=(
            P(None, None, "date", "group"),
            P("date", "group"),
            P(None, None, "date", "group"),
            P(None, "date", "group"),
            P("group"),
            P(),
            P(),
            P(),
            P(),
            P(),
            P(),
            P(),
            P(),
            P(),
            P(),
            P(),
            P(),
            P(),
            P(),
            P(),
        ),
        out_specs=P(None, ("group", "date"), None),
        check_vma=False,
    )
```

profile of v0, /device:TPU:1, one launch (start us, length us, event | category | flops | bytes accessed | tf_op | source)
XLA Modules:
  0.0 717.9 jit_solution(4149455353189141042)
XLA Ops:
  23.4 425.2 %while.26 = (s32[]{:T(128)}, f32[16,128,512]{1,0,2:T(8,128)}, f32[16,128,512]{1,0,2:T(8,128)}, f32[16,512]{1,0:T(8,128)S(1)}, bf16[16,13,24,512]{3,2,1,0:T(8,128...) while((s32[]{:T(128)}, f32[16,128,512]{1,0,2:T(8,128)}, ...), condition=%wide.region_4.5_spmd.clone, body=%wide.region_0.4_spmd.clone.sunk | while | flops 121433600 | bytes 16735827 | solution.py:138
  33.8 8.1 %dynamic_update_slice.24 = f32[16,128,512]{1,0,2:T(8,128)} dynamic-update-slice(f32[16,128,512]{1,0,2:T(8,128)} %get-tuple-element.399, f32[1,128,512]{1,0,2:T(1,128)S(1)} %bitcast.156, s32[]{:T(128)} %get-tuple-element.398, s32[]{:T(128)} %constant.45.clone.1..sunk, s32[]{:T(128)} %constant.45.clone.1..sunk) | dynamic-update-slice | bytes 524292 | tf_op jit(solution)/shard_map/while/body/jit(dynamic_update_index_in_dim)/dynamic_update_slice | solution.py:138
  41.9 8.0 %dynamic_update_slice.25 = f32[16,128,512]{1,0,2:T(8,128)} dynamic-update-slice(f32[16,128,512]{1,0,2:T(8,128)} %get-tuple-element.400, f32[1,128,512]{1,0,2:T(1,128)S(1)} %bitcast.155, s32[]{:T(128)} %get-tuple-element.398, s32[]{:T(128)} %constant.45.clone.1..sunk, s32[]{:T(128)} %constant.45.clone.1..sunk) | dynamic-update-slice | bytes 524292 | tf_op jit(solution)/shard_map/while/body/jit(dynamic_update_index_in_dim)/dynamic_update_slice | solution.py:138
  60.4 8.1 %dynamic_update_slice.24 = f32[16,128,512]{1,0,2:T(8,128)} dynamic-update-slice(f32[16,128,512]{1,0,2:T(8,128)} %get-tuple-element.399, f32[1,128,512]{1,0,2:T(1,128)S(1)} %bitcast.156, s32[]{:T(128)} %get-tuple-element.398, s32[]{:T(128)} %constant.45.clone.1..sunk, s32[]{:T(128)} %constant.45.clone.1..sunk) | dynamic-update-slice | bytes 524292 | tf_op jit(solution)/shard_map/while/body/jit(dynamic_update_index_in_dim)/dynamic_update_slice | solution.py:138
  68.4 8.0 %dynamic_update_slice.25 = f32[16,128,512]{1,0,2:T(8,128)} dynamic-update-slice(f32[16,128,512]{1,0,2:T(8,128)} %get-tuple-element.400, f32[1,128,512]{1,0,2:T(1,128)S(1)} %bitcast.155, s32[]{:T(128)} %get-tuple-element.398, s32[]{:T(128)} %constant.45.clone.1..sunk, s32[]{:T(128)} %constant.45.clone.1..sunk) | dynamic-update-slice | bytes 524292 | tf_op jit(solution)/shard_map/while/body/jit(dynamic_update_index_in_dim)/dynamic_update_slice | solution.py:138
  87.0 8.1 %dynamic_update_slice.24 = f32[16,128,512]{1,0,2:T(8,128)} dynamic-update-slice(f32[16,128,512]{1,0,2:T(8,128)} %get-tuple-element.399, f32[1,128,512]{1,0,2:T(1,128)S(1)} %bitcast.156, s32[]{:T(128)} %get-tuple-element.398, s32[]{:T(128)} %constant.45.clone.1..sunk, s32[]{:T(128)} %constant.45.clone.1..sunk) | dynamic-update-slice | bytes 524292 | tf_op jit(solution)/shard_map/while/body/jit(dynamic_update_index_in_dim)/dynamic_update_slice | solution.py:138
  95.0 8.0 %dynamic_update_slice.25 = f32[16,128,512]{1,0,2:T(8,128)} dynamic-update-slice(f32[16,128,512]{1,0,2:T(8,128)} %get-tuple-element.400, f32[1,128,512]{1,0,2:T(1,128)S(1)} %bitcast.155, s32[]{:T(128)} %get-tuple-element.398, s32[]{:T(128)} %constant.45.clone.1..sunk, s32[]{:T(128)} %constant.45.clone.1..sunk) | dynamic-update-slice | bytes 524292 | tf_op jit(solution)/shard_map/while/body/jit(dynamic_update_index_in_dim)/dynamic_update_slice | solution.py:138
  113.5 8.1 %dynamic_update_slice.24 = f32[16,128,512]{1,0,2:T(8,128)} dynamic-update-slice(f32[16,128,512]{1,0,2:T(8,128)} %get-tuple-element.399, f32[1,128,512]{1,0,2:T(1,128)S(1)} %bitcast.156, s32[]{:T(128)} %get-tuple-element.398, s32[]{:T(128)} %constant.45.clone.1..sunk, s32[]{:T(128)} %constant.45.clone.1..sunk) | dynamic-update-slice | bytes 524292 | tf_op jit(solution)/shard_map/while/body/jit(dynamic_update_index_in_dim)/dynamic_update_slice | solution.py:138
  121.6 8.0 %dynamic_update_slice.25 = f32[16,128,512]{1,0,2:T(8,128)} dynamic-update-slice(f32[16,128,512]{1,0,2:T(8,128)} %get-tuple-element.400, f32[1,128,512]{1,0,2:T(1,128)S(1)} %bitcast.155, s32[]{:T(128)} %get-tuple-element.398, s32[]{:T(128)} %constant.45.clone.1..sunk, s32[]{:T(128)} %constant.45.clone.1..sunk) | dynamic-update-slice | bytes 524292 | tf_op jit(solution)/shard_map/while/body/jit(dynamic_update_index_in_dim)/dynamic_update_slice | solution.py:138
  140.1 8.1 %dynamic_update_slice.24 = f32[16,128,512]{1,0,2:T(8,128)} dynamic-update-slice(f32[16,128,512]{1,0,2:T(8,128)} %get-tuple-element.399, f32[1,128,512]{1,0,2:T(1,128)S(1)} %bitcast.156, s32[]{:T(128)} %get-tuple-element.398, s32[]{:T(128)} %constant.45.clone.1..sunk, s32[]{:T(128)} %constant.45.clone.1..sunk) | dynamic-update-slice | bytes 524292 | tf_op jit(solution)/shard_map/while/body/jit(dynamic_update_index_in_dim)/dynamic_update_slice | solution.py:138
  166.7 8.1 %dynamic_update_slice.24 = f32[16,128,512]{1,0,2:T(8,128)} dynamic-update-slice(f32[16,128,512]{1,0,2:T(8,128)} %get-tuple-element.399, f32[1,128,512]{1,0,2:T(1,128)S(1)} %bitcast.156, s32[]{:T(128)} %get-tuple-element.398, s32[]{:T(128)} %constant.45.clone.1..sunk, s32[]{:T(128)} %constant.45.clone.1..sunk) | dynamic-update-slice | bytes 524292 | tf_op jit(solution)/shard_map/while/body/jit(dynamic_update_index_in_dim)/dynamic_update_slice | solution.py:138
  193.3 8.1 %dynamic_update_slice.24 = f32[16,128,512]{1,0,2:T(8,128)} dynamic-update-slice(f32[16,128,512]{1,0,2:T(8,128)} %get-tuple-element.399, f32[1,128,512]{1,0,2:T(1,128)S(1)} %bitcast.156, s32[]{:T(128)} %get-tuple-element.398, s32[]{:T(128)} %constant.45.clone.1..sunk, s32[]{:T(128)} %constant.45.clone.1..sunk) | dynamic-update-slice | bytes 524292 | tf_op jit(solution)/shard_map/while/body/jit(dynamic_update_index_in_dim)/dynamic_update_slice | solution.py:138
  219.8 8.1 %dynamic_update_slice.24 = f32[16,128,512]{1,0,2:T(8,128)} dynamic-update-slice(f32[16,128,512]{1,0,2:T(8,128)} %get-tuple-element.399, f32[1,128,512]{1,0,2:T(1,128)S(1)} %bitcast.156, s32[]{:T(128)} %get-tuple-element.398, s32[]{:T(128)} %constant.45.clone.1..sunk, s32[]{:T(128)} %constant.45.clone.1..sunk) | dynamic-update-slice | bytes 524292 | tf_op jit(solution)/shard_map/while/body/jit(dynamic_update_index_in_dim)/dynamic_update_slice | solution.py:138
  246.4 8.1 %dynamic_update_slice.24 = f32[16,128,512]{1,0,2:T(8,128)} dynamic-update-slice(f32[16,128,512]{1,0,2:T(8,128)} %get-tuple-element.399, f32[1,128,512]{1,0,2:T(1,128)S(1)} %bitcast.156, s32[]{:T(128)} %get-tuple-element.398, s32[]{:T(128)} %constant.45.clone.1..sunk, s32[]{:T(128)} %constant.45.clone.1..sunk) | dynamic-update-slice | bytes 524292 | tf_op jit(solution)/shard_map/while/body/jit(dynamic_update_index_in_dim)/dynamic_update_slice | solution.py:138
  273.0 8.1 %dynamic_update_slice.24 = f32[16,128,512]{1,0,2:T(8,128)} dynamic-update-slice(f32[16,128,512]{1,0,2:T(8,128)} %get-tuple-element.399, f32[1,128,512]{1,0,2:T(1,128)S(1)} %bitcast.156, s32[]{:T(128)} %get-tuple-element.398, s32[]{:T(128)} %constant.45.clone.1..sunk, s32[]{:T(128)} %constant.45.clone.1..sunk) | dynamic-update-slice | bytes 524292 | tf_op jit(solution)/shard_map/while/body/jit(dynamic_update_index_in_dim)/dynamic_update_slice | solution.py:138
  299.6 8.1 %dynamic_update_slice.24 = f32[16,128,512]{1,0,2:T(8,128)} dynamic-update-slice(f32[16,128,512]{1,0,2:T(8,128)} %get-tuple-element.399, f32[1,128,512]{1,0,2:T(1,128)S(1)} %bitcast.156, s32[]{:T(128)} %get-tuple-element.398, s32[]{:T(128)} %constant.45.clone.1..sunk, s32[]{:T(128)} %constant.45.clone.1..sunk) | dynamic-update-slice | bytes 524292 | tf_op jit(solution)/shard_map/while/body/jit(dynamic_update_index_in_dim)/dynamic_update_slice | solution.py:138
  326.1 8.1 %dynamic_update_slice.24 = f32[16,128,512]{1,0,2:T(8,128)} dynamic-update-slice(f32[16,128,512]{1,0,2:T(8,128)} %get-tuple-element.399, f32[1,128,512]{1,0,2:T(1,128)S(1)} %bitcast.156, s32[]{:T(128)} %get-tuple-element.398, s32[]{:T(128)} %constant.45.clone.1..sunk, s32[]{:T(128)} %constant.45.clone.1..sunk) | dynamic-update-slice | bytes 524292 | tf_op jit(solution)/shard_map/while/body/jit(dynamic_update_index_in_dim)/dynamic_update_slice | solution.py:138
  352.7 8.1 %dynamic_update_slice.24 = f32[16,128,512]{1,0,2:T(8,128)} dynamic-update-slice(f32[16,128,512]{1,0,2:T(8,128)} %get-tuple-element.399, f32[1,128,512]{1,0,2:T(1,128)S(1)} %bitcast.156, s32[]{:T(128)} %get-tuple-element.398, s32[]{:T(128)} %constant.45.clone.1..sunk, s32[]{:T(128)} %constant.45.clone.1..sunk) | dynamic-update-slice | bytes 524292 | tf_op jit(solution)/shard_map/while/body/jit(dynamic_update_index_in_dim)/dynamic_update_slice | solution.py:138
  379.3 8.1 %dynamic_update_slice.24 = f32[16,128,512]{1,0,2:T(8,128)} dynamic-update-slice(f32[16,128,512]{1,0,2:T(8,128)} %get-tuple-element.399, f32[1,128,512]{1,0,2:T(1,128)S(1)} %bitcast.156, s32[]{:T(128)} %get-tuple-element.398, s32[]{:T(128)} %constant.45.clone.1..sunk, s32[]{:T(128)} %constant.45.clone.1..sunk) | dynamic-update-slice | bytes 524292 | tf_op jit(solution)/shard_map/while/body/jit(dynamic_update_index_in_dim)/dynamic_update_slice | solution.py:138
  405.9 8.1 %dynamic_update_slice.24 = f32[16,128,512]{1,0,2:T(8,128)} dynamic-update-slice(f32[16,128,512]{1,0,2:T(8,128)} %get-tuple-element.399, f32[1,128,512]{1,0,2:T(1,128)S(1)} %bitcast.156, s32[]{:T(128)} %get-tuple-element.398, s32[]{:T(128)} %constant.45.clone.1..sunk, s32[]{:T(128)} %constant.45.clone.1..sunk) | dynamic-update-slice | bytes 524292 | tf_op jit(solution)/shard_map/while/body/jit(dynamic_update_index_in_dim)/dynamic_update_slice | solution.py:138
  432.4 8.1 %dynamic_update_slice.24 = f32[16,128,512]{1,0,2:T(8,128)} dynamic-update-slice(f32[16,128,512]{1,0,2:T(8,128)} %get-tuple-element.399, f32[1,128,512]{1,0,2:T(1,128)S(1)} %bitcast.156, s32[]{:T(128)} %get-tuple-element.398, s32[]{:T(128)} %constant.45.clone.1..sunk, s32[]{:T(128)} %constant.45.clone.1..sunk) | dynamic-update-slice | bytes 524292 | tf_op jit(solution)/shard_map/while/body/jit(dynamic_update_index_in_dim)/dynamic_update_slice | solution.py:138
  473.4 8.8 %all-to-all-start = ((bf16[16,32,16,256]{3,0,2,1:T(8,128)(2,1)}), bf16[16,32,16,256]{3,0,2,1:T(8,128)(2,1)}, u32[]{:S(2)}, u32[]{:S(2)}) async-start(bf16[16,32,16,256]{3,0,2,1:T(8,128)(2,1)} %bitcast.158), calls=%async_computation | async-start | bytes 8388608 | tf_op jit(solution)/shard_map/all_to_all | solution.py:159
  483.4 51.1 %all-to-all-done = bf16[16,32,16,256]{3,0,2,1:T(8,128)(2,1)} async-done(((bf16[16,32,16,256]{3,0,2,1:T(8,128)(2,1)}), bf16[16,32,16,256]{3,0,2,1:T(8,128)(2,1)}, u32[]{:S(2)}, u32[]{:S(2)}) %all-to-all-start) | async-done | bytes 4194336 | tf_op jit(solution)/shard_map/all_to_all | solution.py:159
  538.6 174.9 %while.25 = (s32[]{:T(128)}, bf16[16,512,128]{1,2,0:T(8,128)(2,1)}, bf16[16,512,128]{2,1,0:T(8,128)(2,1)S(1)}, f32[128]{0:T(128)S(1)}, bf16[128,128]{1,0:T(8,128...) while((s32[]{:T(128)}, bf16[16,512,128]{1,2,0:T(8,128)(2,1)}, ...), condition=%wide.region_18.19_spmd, body=%wide.region_11.18_spmd.sunk | while | flops 360252928 | bytes 12384889 | solution.py:96
  (483 shorter events, 494.7 us)
Async XLA Ops:
  0.0 537.2 %copy-start = (bf16[256,128]{1,0:T(8,128)(2,1)S(1)}, bf16[256,128]{1,0:T(8,128)(2,1)}, u32[]{:S(2)}) copy-start(bf16[256,128]{1,0:T(8,128)(2,1)} %param.34) | copy-start | bytes 196612
  2.4 11.6 %copy-start.3 = (s32[8,16,64]{2,1,0:T(8,128)S(1)}, s32[8,16,64]{2,1,0:T(8,128)}, u32[]{:S(2)}) copy-start(s32[8,16,64]{2,1,0:T(8,128)} %param.27) | copy-start | bytes 98308
  9.8 440.3 %collective-permute-start = (f32[128,16,64]{0,2,1:T(8,128)S(1)}, f32[128,16,64]{0,2,1:T(8,128)S(1)}, u32[]{:S(2)}, u32[]{:S(2)}) collective-permute-start(f32[128,16,64]{0,2,1:T(8,128)S(1)} %bitcast.163), channel_id=1, source_target_pairs={{224,0},{0,32},{32,64},{64,96},{96,128},{128,160},{160,192},{192,2... | collective-permute-start | bytes 1572872 | tf_op jit(solution)/shard_map/ppermute | solution.py:18
  12.3 438.1 %collective-permute-start.2 = (f32[128,16,64]{0,2,1:T(8,128)S(1)}, f32[128,16,64]{0,2,1:T(8,128)S(1)}, u32[]{:S(2)}, u32[]{:S(2)}) collective-permute-start(f32[128,16,64]{0,2,1:T(8,128)S(1)} %bitcast.162), channel_id=1, source_target_pairs={{224,0},{0,32},{32,64},{64,96},{96,128},{128,160},{160,192},{192,2... | collective-permute-start | bytes 1572872 | tf_op jit(solution)/shard_map/ppermute | solution.py:18
  14.0 434.8 %collective-permute-start.1 = (f32[16,64]{1,0:T(8,128)S(1)}, f32[16,64]{1,0:T(8,128)S(1)}, u32[]{:S(2)}, u32[]{:S(2)}) collective-permute-start(f32[16,64]{1,0:T(8,128)S(1)} %convert_reduce_fusion.1), channel_id=1, source_target_pairs={{224,0},{0,32},{32,64},{64,96},{96,128},{128,160},{160,192},{192,2... | collective-permute-start | bytes 12296 | tf_op jit(solution)/shard_map/ppermute | solution.py:18
  15.7 7.7 %copy-start.2 = (bf16[128,32]{0,1:T(8,128)(2,1)S(1)}, bf16[128,32]{0,1:T(8,128)(2,1)}, u32[]{:S(2)}) copy-start(bf16[128,32]{0,1:T(8,128)(2,1)} %param.32) | copy-start | bytes 24580
  15.7 7.7 %copy-start.4 = (bf16[32,13]{0,1:T(8,128)(2,1)S(1)}, bf16[32,13]{0,1:T(8,128)(2,1)}, u32[]{:S(2)}) copy-start(bf16[32,13]{0,1:T(8,128)(2,1)} %param.30) | copy-start | bytes 2500
  15.7 7.7 %copy-start.5 = (f32[32]{0:T(128)S(1)}, f32[32]{0:T(128)}, u32[]{:S(2)}) copy-start(f32[32]{0:T(128)} %param.31) | copy-start | bytes 388
  15.7 7.7 %copy-start.6 = (f32[128]{0:T(128)S(1)}, f32[128]{0:T(128)}, u32[]{:S(2)}) copy-start(f32[128]{0:T(128)} %param.33) | copy-start | bytes 1540
  23.4 425.2 %copy-start.14 = (s32[64]{0:T(128)S(1)}, s32[64]{0:T(128)}, u32[]{:S(2)}) copy-start(s32[64]{0:T(128)} %param.28) | copy-start | bytes 772
  473.4 8.8 %copy-start.7 = (s32[512]{0:T(512)S(1)}, s32[512]{0:T(512)}, u32[]{:S(2)}) copy-start(s32[512]{0:T(512)} %param.29) | copy-start | bytes 6148
  473.4 61.0 %all-to-all-start = ((bf16[16,32,16,256]{3,0,2,1:T(8,128)(2,1)}), bf16[16,32,16,256]{3,0,2,1:T(8,128)(2,1)}, u32[]{:S(2)}, u32[]{:S(2)}) async-start(bf16[16,32,16,256]{3,0,2,1:T(8,128)(2,1)} %bitcast.158), calls=%async_computation | async-start | bytes 8388608 | tf_op jit(solution)/shard_map/all_to_all | solution.py:159
  534.5 2.8 copy-start.8
  537.1 1.4 copy-start.1
  537.1 1.4 copy-start.9
  537.1 1.4 copy-start.10
  537.1 1.4 copy-start.11
  537.2 1.4 copy-start.12
  537.2 1.4 copy-start.13
  537.2 1.4 copy-start.15
  537.2 1.4 copy-start.16
where the time goes:
time: 729 us; the launch traced here: 718 us
  local copies, waits for them, and re-layouts  308 us (42%)
  matrix products  238 us (33%)
  other arithmetic  104 us (14%)
  waiting for transfers between devices  51.1 us (7%)
  starting transfers between devices  14.7 us (2%)
    dynamic_update_slice x48, local copies, waits for them, and re-layouts, per_device(): lax.map(per_date, (jnp.moveaxis(pixels, 2, 0), counts))  259 us
    reduce_sum x16, other arithmetic, pixel_stats(): jnp.sum(weighted * h_two, axis=1)  71.3 us
    dot_general x17, matrix products, pixel_stats(): jnp.dot(w_second, h_one, preferred_element_type=jnp.float32)  67.8 us
    dot_general x16, matrix products, temporal_layer(): jnp.dot(hidden, w_down, preferred_element_type=jnp.float32)  55.5 us
    sub x16, matrix products, temporal_layer(): att_weights = jax.nn.softmax(scores, axis=-1).astype(jnp.bfloat16)  54.9 us
    all_to_all x1, waiting for transfers between devices, per_device(): lax.all_to_all(payload, 'date', split_axis=1, concat_axis=0, tiled=True)  51.1 us
    dot_general x16, matrix products, temporal_layer(): jnp.einsum('hqk,khd->qhd', att_weights, values, preferred_element_type=jn...  42.8 us
    while x48, local copies, waits for them, and re-layouts  18.3 us
  transfers between devices with their start and end apart: 4, of which 1 were waited for; matrix products, arithmetic and copies ran while one was open for 61% of the time, Pallas kernels for 0%

commit v1 on v0

v1 whole, which is shorter than its diff:
```python
import functools
import math

import jax
import jax.numpy as jnp
from jax import lax
from jax.experimental import pallas as pl
from jax.experimental.pallas import tpu as pltpu
from jax.sharding import PartitionSpec as P

HEADS = 4
VAR_FLOOR = 0.05
NORM_EPS = 1e-05
F32 = jnp.float32
BF16 = jnp.bfloat16
LANES = 128


def three_parts(values):
    high = lax.reduce_precision(values, 8, 7)
    rest = values - high
    middle = lax.reduce_precision(rest, 8, 7)
    low = rest - middle
    return high.astype(BF16), middle.astype(BF16), low.astype(BF16)


def pixel_weights(w_first, b_first, w_second, b_second, dates):
    h1, bands = w_first.shape
    feats = w_second.shape[0]
    same = jnp.eye(dates, dtype=BF16)
    first = (w_first.T[:, None, None, :] * same[None, :, :, None]).reshape(bands * dates, dates * h1)
    bias = jnp.stack(three_parts(b_first))
    bias = (bias[:, None, None, :] * same[None, :, :, None]).reshape(3 * dates, dates * h1)
    first = jnp.concatenate([first, bias], axis=0)
    pairs = dates // 2
    place = jnp.arange(pairs)
    dates_in = jnp.arange(4)
    dates_out = jnp.arange(2)
    hit = (dates_in[None, :, None] == (2 * (place % 2))[:, None, None] + dates_out[None, None, :]).astype(BF16)
    second = (hit[:, :, None, :, None] * w_second.T[None, None, :, None, :]).reshape(pairs, 4 * h1, 2 * feats)
    bias = jnp.stack(three_parts(b_second))
    absolute = (jnp.arange(dates)[None, :, None] == 2 * place[:, None, None] + dates_out[None, None, :]).astype(BF16)
    tail = (absolute[:, None, :, :, None] * bias[None, :, None, None, :]).reshape(pairs, 3 * dates, 2 * feats)
    gap = jnp.zeros((pairs, LANES - 3 * dates, 2 * feats), BF16)
    return first, jnp.concatenate([second, gap, tail], axis=1)


def relu_bf16(values):
    return jnp.maximum(values, 0.0).astype(BF16)


def pixel_kernel(
    pix_ref, cnt_ref, edge_ref, lot_ref, w1_ref, w2_ref, wp_ref, code_ref, perm_ref, out_ref,
    xt_ref, h_ref, es_ref, ec_ref, init_ref, inv_ref, pool_ref, e_ref,
):
    bands, slots, dates, lots = pix_ref.shape
    edge_slots = edge_ref.shape[1]
    pairs = w2_ref.shape[0]
    block = pl.program_id(0)
    rows = lots // 4

    def one_slot(p, source, mask, count):
        x = jnp.concatenate([source(b) for b in range(bands)] + [mask] * 3, axis=0)
        xt = x.T
        for r in range(4):
            xt_ref[r, pl.ds(p * rows, rows), :] = xt[r * rows : (r + 1) * rows]

    def first_layer(count):
        for r in range(4):
            z = jnp.dot(xt_ref[r, : count * rows, :], w1_ref[...], preferred_element_type=F32)
            z = relu_bf16(z)
            for g in range(4):
                h_ref[g, r, : count * rows, :] = z[:, g * LANES : (g + 1) * LANES]

    def second_layer(j, r, count):
        a = jnp.concatenate(
            [h_ref[j // 2, r, : count * rows, :], xt_ref[r, : count * rows, LANES:]], axis=1
        )
        z = jnp.dot(a, w2_ref[j], preferred_element_type=F32)
        total = square = None
        for p in range(count):
            part = jnp.maximum(z[p * rows : (p + 1) * rows], 0.0)
            total = part if total is None else total + part
            square = part * part if square is None else square + part * part
        return total, square

    @pl.when(block == 0)
    def _():
        half = lots // 2
        ec = jnp.zeros((dates, lots), F32)
        for p in range(edge_slots):
            mask = edge_ref[bands, p]
            one_slot(p, lambda b: edge_ref[b, p], mask, edge_slots)
            ec = ec + mask.astype(F32)
        ec_ref[...] = ec.astype(BF16)
        first_layer(edge_slots)
        es_ref[...] = jnp.zeros_like(es_ref)

        @pl.loop(0, pairs)
        def _(j):
            stats = [second_layer(j, r, edge_slots) for r in range(4)]
            for k in range(2):
                for r in range(2):
                    v = stats[r][k] + stats[r + 2][k]
                    for part in range(3):
                        cut = v.astype(BF16)
                        es_ref[j, pl.ds(part * half + r * rows, rows), 256 * k : 256 * (k + 1)] = cut
                        v = v - cut.astype(F32)

    counts = cnt_ref[...]
    for p in range(slots):
        mask = jnp.where(counts > p, 1.0, 0.0).astype(BF16)
        one_slot(p, lambda b: pix_ref[b, p] * mask, mask, slots)
    first_layer(slots)

    lot = lot_ref[...]
    lot_ids = lax.broadcasted_iota(jnp.int32, (lots, 256), 0) + block * lots
    chosen = jnp.where(lot_ids == lot, 1.0, 0.0).astype(BF16)
    lot_rows = lax.broadcasted_iota(jnp.int32, (lots, lots), 0) + block * lots
    chosen_twice = jnp.where(lot_rows == lot[:, :lots], 1.0, 0.0).astype(BF16)
    extra = lax.dot_general(ec_ref[...], chosen_twice, (((1,), (1,)), ((), ())), preferred_element_type=F32)
    inverse = 1.0 / (counts.astype(F32) + extra)
    inv_t = inverse.T
    for d in range(dates):
        inv_ref[d] = jnp.broadcast_to(inv_t[:, d : d + 1], (lots, LANES))

    @pl.loop(0, pairs)
    def _(j):
        init_ref[...] = jnp.dot(chosen, es_ref[j], preferred_element_type=F32)
        for r in range(4):
            total, square = second_layer(j, r, slots)
            here = slice(r * rows, (r + 1) * rows)
            total = total + init_ref[here, :256]
            square = square + init_ref[here, 256:]
            for k in range(2):
                inv = inv_ref[2 * j + k, here, :]
                lanes = slice(k * LANES, (k + 1) * LANES)
                average = total[:, lanes] * inv
                spread = jnp.maximum(square[:, lanes] * inv - average * average, VAR_FLOOR)
                spread = spread * lax.rsqrt(spread)
                pool_ref[2 * j + k, here, :LANES] = average.astype(BF16)
                pool_ref[2 * j + k, here, LANES:] = spread.astype(BF16)

    for d in range(dates):
        e = jnp.dot(pool_ref[d], wp_ref[...], preferred_element_type=F32) + code_ref[d : d + 1, :]
        e_ref[d] = e.astype(BF16)
    own = out_ref.shape[1]
    for k in range(0, lots // own, 2):
        both = jnp.concatenate(
            [e_ref[:, (k + s) * own : (k + s + 1) * own, :].reshape(dates * own, LANES) for s in range(2)], axis=1
        )
        y = jnp.dot(perm_ref[...], both, preferred_element_type=F32).astype(BF16)
        for s in range(2):
            out_ref[k + s] = y[:, s * LANES : (s + 1) * LANES].reshape(own, dates, LANES)


def pool_lots(pixels, counts, edges, lots_owned, w1, w2, w_pool, code, perm, peers):
    bands, slots, dates, lots = pixels.shape
    own = lots // peers
    block = LANES
    feats = w_pool.shape[1]
    pairs = dates // 2
    whole = lambda shape: pl.BlockSpec(shape, lambda i: (0,) * len(shape), pipeline_mode=pl.Buffered(1))
    return pl.pallas_call(
        pixel_kernel,
        grid=(lots // block,),
        in_specs=[
            pl.BlockSpec((bands, slots, dates, block), lambda i: (0, 0, 0, i)),
            pl.BlockSpec((dates, block), lambda i: (0, i)),
            whole(edges.shape),
            whole(lots_owned.shape),
            whole(w1.shape),
            whole(w2.shape),
            whole(w_pool.shape),
            whole(code.shape),
            whole(perm.shape),
        ],
        out_specs=pl.BlockSpec((block // own, own, dates, feats), lambda i: (i, 0, 0, 0)),
        out_shape=jax.ShapeDtypeStruct((peers, own, dates, feats), BF16),
        scratch_shapes=[
            pltpu.VMEM((4, slots * block // 4, 256), BF16),
            pltpu.VMEM((4, 4, slots * block // 4, LANES), BF16),
            pltpu.VMEM((pairs, 256, 512), BF16),
            pltpu.VMEM((dates, block), BF16),
            pltpu.VMEM((block, 512), F32),
            pltpu.VMEM((dates, block, LANES), F32),
            pltpu.VMEM((dates, block, 256), BF16),
            pltpu.VMEM((dates, block, LANES), BF16),
        ],
        compiler_params=pltpu.CompilerParams(vmem_limit_bytes=48 << 20),
        name="pixel_pool",
    )(pixels, counts, edges, lots_owned, w1, w2, w_pool, code, perm)


def erf_gelu(x):
    return 0.5 * x * (1.0 + lax.erf(x * (1.0 / math.sqrt(2.0))))


def norm_rows(x, gain):
    average = jnp.mean(x, axis=-1, keepdims=True)
    centered = x - average
    variance = jnp.mean(centered * centered, axis=-1, keepdims=True)
    return centered * lax.rsqrt(variance + NORM_EPS) * gain


def attention_kernel(
    e_ref, ln1_ref, wqk_ref, wvt_ref, wo_ref, ln2_ref, up_ref, down_ref, perm_ref, out_ref, enc_ref
):
    peers, own, dates, width = e_ref.shape
    total = peers * dates
    head = width // HEADS
    lane = lax.broadcasted_iota(jnp.int32, (total, width), 1)
    scale = math.log2(math.e) / math.sqrt(head)

    @pl.loop(0, own)
    def _(lot):
        series = e_ref[:, lot].reshape(total, width).astype(F32)
        normed = norm_rows(series, ln1_ref[...]).astype(BF16)
        both = jnp.dot(normed, wqk_ref[...], preferred_element_type=F32).astype(BF16)
        queries = both[:, :width]
        keys = both[:, width:]
        values_t = lax.dot_general(
            wvt_ref[...], normed, (((1,), (1,)), ((), ())), preferred_element_type=F32
        ).astype(BF16)
        ones = jnp.ones((16, total), BF16)
        mixed = []
        for h in range(HEADS):
            mine = jnp.where(lane // head == h, queries, jnp.zeros_like(queries))
            scores = lax.dot_general(keys, mine, (((1,), (1,)), ((), ())), preferred_element_type=F32)
            top = jnp.max(scores, axis=0, keepdims=True) * scale
            weights = jnp.exp2(scores * scale - top).astype(BF16)
            lhs = jnp.concatenate([values_t[h * head : (h + 1) * head], ones], axis=0)
            mix = jnp.dot(lhs, weights, preferred_element_type=F32)
            mixed.append((mix[:head] * (1.0 / mix[head : head + 1])).astype(BF16))
        mixture = jnp.concatenate(mixed, axis=0).T
        carried = series + jnp.dot(mixture, wo_ref[...], preferred_element_type=F32)
        normed_two = norm_rows(carried, ln2_ref[...]).astype(BF16)
        hidden = erf_gelu(jnp.dot(normed_two, up_ref[...], preferred_element_type=F32)).astype(BF16)
        encoded = carried + jnp.dot(hidden, down_ref[...], preferred_element_type=F32)
        enc_ref[lot] = encoded.astype(BF16).reshape(peers, dates, width)

    for p in range(0, peers, 2):
        two = jnp.concatenate([enc_ref[:, p + s].reshape(own * dates, width) for s in range(2)], axis=1)
        y = jnp.dot(perm_ref[...], two, preferred_element_type=F32).astype(BF16)
        for s in range(2):
            out_ref[pl.ds((p + s) * dates, dates)] = y[:, s * width : (s + 1) * width].reshape(dates, own, width)


def attend(embedded, ln1, wqk, wvt, wo, ln2, up, down, perm):
    peers, own, dates, width = embedded.shape
    return pl.pallas_call(
        attention_kernel,
        out_shape=jax.ShapeDtypeStruct((peers * dates, own, width), BF16),
        scratch_shapes=[pltpu.VMEM((own, peers, dates, width), BF16)],
        compiler_params=pltpu.CompilerParams(vmem_limit_bytes=56 << 20),
        name="attend",
    )(embedded, ln1, wqk, wvt, wo, ln2, up, down, perm)


def position_code(day_numbers, model_width):
    half_ids = jnp.arange(model_width // 2, dtype=F32)
    freq_rate = jnp.exp(-(2.0 * half_ids / model_width) * math.log(1000.0))
    phase_angle = day_numbers.astype(F32)[:, None] * freq_rate[None]
    return jnp.stack([jnp.sin(phase_angle), jnp.cos(phase_angle)], axis=-1).reshape(
        day_numbers.shape[0], model_width
    )


def swap_rows(minor, major):
    row = lax.broadcasted_iota(jnp.int32, (minor * major, minor * major), 0)
    col = lax.broadcasted_iota(jnp.int32, (minor * major, minor * major), 1)
    return (col == (row % minor) * major + row // minor).astype(BF16)


def edge_rows(edge_pixels, edge_mask):
    half = edge_pixels.shape[1] // 2
    mask = edge_mask.astype(BF16)
    rows = jnp.concatenate([edge_pixels * mask[None], mask[None]], axis=0)
    return jnp.concatenate([rows[:, :half], rows[:, half:]], axis=-1)


def per_device(
    pixels, counts, edge_pixels, edge_mask, straddle_lot, date_days,
    w_first, b_first, w_second, b_second, w_pool, b_pool,
    ln_one, w_query, w_key, w_value, w_out, ln_two, w_up, w_down,
):
    groups = lax.axis_size("group")
    peers = lax.axis_size("date")
    dates = pixels.shape[2]
    width = w_pool.shape[1]
    edges = lax.ppermute(
        edge_rows(edge_pixels, edge_mask), "group", [(i, (i + 1) % groups) for i in range(groups)]
    )
    w1, w2 = pixel_weights(w_first, b_first, w_second, b_second, dates)
    own_days = lax.dynamic_slice_in_dim(date_days, lax.axis_index("date") * dates, dates)
    code = position_code(own_days, width) + b_pool
    perm = swap_rows(dates, pixels.shape[3] // peers)
    lots_owned = jnp.concatenate([straddle_lot] * 3 + [jnp.full_like(straddle_lot, -1)])[None]
    pooled = pool_lots(pixels, counts, edges, lots_owned, w1, w2, w_pool, code, perm, peers)
    series = lax.all_to_all(pooled, "date", split_axis=0, concat_axis=0, tiled=True)
    wqk = jnp.concatenate([w_query, w_key], axis=1)
    return attend(
        series, ln_one[None], wqk, w_value.T, w_out, ln_two[None], w_up, w_down, perm
    )


def solution(mesh):
    return jax.shard_map(
        per_device,
        mesh=mesh,
        in_specs=(
            P(None, None, "date", "group"),
            P("date", "group"),
            P(None, None, "date", "group"),
            P(None, "date", "group"),
            P("group"),
        )
        + (P(),) * 15,
        out_specs=P(None, ("group", "date"), None),
        check_vma=False,
    )
```

time: 729 us -> 149 us (0.20); the launches traced: 718 us -> 149 us
  local copies, waits for them, and re-layouts: 308 us -> 4.48 us
  matrix products: 238 us -> 0 us
  other arithmetic: 104 us -> 5.6 us
  Pallas kernels: 0 us -> 95.8 us
  waiting for transfers between devices: 51.1 us -> 31.5 us
    dynamic_update_slice x48 -> x0, local copies, waits for them, and re-layouts: 259 us -> none  [per_device(): lax.map(per_date, (jnp.moveaxis(pixels, 2, 0), counts))]
    dot_general x114 -> x0, matrix products: 183 us -> none  [the longest x17 67.8 us: pixel_stats(): jnp.dot(w_second, h_one, preferred_element_type=jnp.float32)]
    pallas_call x0 -> x2, Pallas kernels: none -> 95.8 us  [the longest x1 59.5 us: attend(): pl.pallas_call(attention_kernel, out_shape=jax.ShapeDtypeStruct((peers *...]
    reduce_sum x82 -> x0, other arithmetic: 77.7 us -> none  [the longest x16 71.3 us: pixel_stats(): jnp.sum(weighted * h_two, axis=1)]
    sub x16 -> x0, matrix products: 54.9 us -> none  [temporal_layer(): att_weights = jax.nn.softmax(scores, axis=-1).astype(jnp.bfloat16)]
    all_to_all x1, waiting for transfers between devices: 51.1 us -> 26.9 us  [per_device(): lax.all_to_all(pooled, 'date', split_axis=0, concat_axis=0, tiled=True)]
    while x50 -> x0, local copies, waits for them, and re-layouts: 22.9 us -> none
    scatter-add x3 -> x0, other arithmetic: 16.2 us -> none  [the longest x1 7.5 us: per_device(): sum_all = sum_all.at[:, :, straddle_lot].add(jnp.swapaxes(edge_sum, 0, 1))]
  transfers between devices with their start and end apart: 4 -> 2, of which waited for: 1 -> 2; matrix products, arithmetic and copies ran while one was open for 61% -> 4% of each run, Pallas kernels for 0% -> 0%
where the time goes in v1:
time: 149 us
  Pallas kernels  95.8 us (64%)
  waiting for transfers between devices  31.5 us (21%)
  starting transfers between devices  11 us (7%)
  other arithmetic  5.6 us (4%)
  local copies, waits for them, and re-layouts  4.48 us (3%)
    pallas_call x1, Pallas kernels, attend(): pl.pallas_call(attention_kernel, out_shape=jax.ShapeDtypeStruct((peers *...  59.5 us
    pallas_call x1, Pallas kernels, pool_lots(): pl.pallas_call(pixel_kernel, grid=(lots // block,), in_specs=[pl.BlockSpe...  36.3 us
    all_to_all x1, waiting for transfers between devices, per_device(): lax.all_to_all(pooled, 'date', split_axis=0, concat_axis=0, tiled=True)  26.9 us
    all_to_all x1, starting transfers between devices, per_device(): lax.all_to_all(pooled, 'date', split_axis=0, concat_axis=0, tiled=True)  8.43 us
    ppermute x1, waiting for transfers between devices, per_device(): lax.ppermute(edge_rows(edge_pixels, edge_mask), 'group', [(i, (i + 1) % g...  4.53 us
  transfers between devices with their start and end apart: 2, of which 2 were waited for; matrix products, arithmetic and copies ran while one was open for 4% of the time, Pallas kernels for 0%

profile of v1, /device:TPU:1, one launch (start us, length us, event | category | flops | bytes accessed | tf_op | source)
XLA Modules:
  0.0 148.7 jit_solution(13407754483565548002)
XLA Ops:
  0.0 0.9 convert_element_type.52
  0.9 0.8 convert_bitcast_fusion
  1.7 1.0 broadcast_multiply_fusion.2
  2.8 0.1 fusion.2
  3.0 2.5 %collective-permute-start = (bf16[14,4,16,128]{3,2,1,0:T(8,128)(2,1)S(1)}, bf16[14,4,16,128]{3,2,1,0:T(8,128)(2,1)S(1)}, u32[]{:S(2)}, u32[]{:S(2)}) collective-permute-start(bf16[14,4,16,128]{3,2,1,0:T(8,128)(2,1)S(1)} %fusion.2), channel_id=1, source_target_pairs={{0,32},{32,64},{64,96},{96,128},{128,160},{160,192},{192,224},{224... | collective-permute-start | bytes 688136 | tf_op jit(solution)/shard_map/ppermute | solution.py:291
  5.6 0.8 dynamic-slice_convert_fusion
  6.8 0.2 mul.154
  7.0 0.1 broadcast_multiply_fusion
  7.2 0.8 mul.150
  8.1 0.2 mul.163
  8.3 0.1 mul.164
  8.5 0.3 mul.156
  8.9 0.3 mul.157
  9.5 0.2 pad_maximum_fusion.w2_ref
  9.7 0.2 copy-done.12
  10.0 0.3 fusion.perm_ref
  10.3 4.5 %collective-permute-done.edge_ref = bf16[14,4,16,128]{3,2,1,0:T(8,128)(2,1)S(1)} collective-permute-done((bf16[14,4,16,128]{3,2,1,0:T(8,128)(2,1)S(1)}, bf16[14,4,16,128]{3,2,1,0:T(8,128)(2,1)S(1)}, u32[]{:S(2)}, u32[]{:S(2)}) %collective-permute-start) | collective-permute-done | bytes 229408 | tf_op jit(solution)/shard_map/ppermute | solution.py:291
  14.8 36.3 %pixel_pool.1 = bf16[32,16,16,128]{3,2,1,0:T(8,128)(2,1)} custom-call(bf16[13,24,16,512]{3,2,1,0:T(8,128)(2,1)} %pix_ref.1, s32[16,512]{1,0:T(8,128)S(1)} %copy-done.2, bf16[14,4,16,128]{3,2,1,0:T(8,128)(2,1)S(1)} %collective-permute-done.edge_ref, s32[1,256]{1,0:T(1,128)S(1)} %bitcast.35, bf16[256,512]{1,0:T(8,128)(2,1)S(1)} %pad_maximum_fusion.1.w1_ref, ...), custom_call_target="tpu_custom_call" | custom-call | tf_op jit(solution)/shard_map/pixel_pool/pallas_call | solution.py:164
  51.1 8.4 %all-to-all-start = ((bf16[32,16,16,128]{3,2,1,0:T(8,128)(2,1)}), bf16[32,16,16,128]{3,2,1,0:T(8,128)(2,1)S(1)}, u32[]{:S(2)}, u32[]{:S(2)}) async-start(bf16[32,16,16,128]{3,2,1,0:T(8,128)(2,1)} %pixel_pool.1), calls=%async_computation | async-start | bytes 4194304 | tf_op jit(solution)/shard_map/all_to_all | solution.py:300
  59.5 0.7 copy.26
  60.2 0.6 pad_maximum_fusion.3.wqk_ref
  60.9 26.9 %all-to-all-done.e_ref = bf16[32,16,16,128]{3,2,1,0:T(8,128)(2,1)S(1)} async-done(((bf16[32,16,16,128]{3,2,1,0:T(8,128)(2,1)}), bf16[32,16,16,128]{3,2,1,0:T(8,128)(2,1)S(1)}, u32[]{:S(2)}, u32[]{:S(2)}) %all-to-all-start) | async-done | bytes 2097184 | tf_op jit(solution)/shard_map/all_to_all | solution.py:300
  87.8 1.3 copy-done.3
  89.2 59.5 %attend.1 = bf16[512,16,128]{2,1,0:T(8,128)(2,1)} custom-call(bf16[32,16,16,128]{3,2,1,0:T(8,128)(2,1)} %copy-done.3, f32[1,128]{1,0:T(1,128)} %bitcast.44, bf16[128,256]{1,0:T(8,128)(2,1)} %pad_maximum_fusion.3.wqk_ref, bf16[128,128]{1,0:T(8,128)(2,1)} %bitcast.39, bf16[128,128]{1,0:T(8,128)(2,1)} %wo_ref.1, f32[1,128]{1,0:T(1,128)} %bitcast.45, ...), custom_call_target="tpu_custom_call" | custom-call | tf_op jit(solution)/shard_map/attend/pallas_call | solution.py:251
  (57 shorter events, 1.0 us)
Async XLA Ops:
  0.0 6.6 %copy-start.10 = (f32[32]{0:T(128)S(1)}, f32[32]{0:T(128)}, u32[]{:S(2)}) copy-start(f32[32]{0:T(128)} %param.27) | copy-start | bytes 388
  0.0 7.0 %copy-start.8 = (bf16[32,13]{0,1:T(8,128)(2,1)S(1)}, bf16[32,13]{0,1:T(8,128)(2,1)}, u32[]{:S(2)}) copy-start(bf16[32,13]{0,1:T(8,128)(2,1)} %param.26) | copy-start | bytes 2500
  2.8 5.2 %copy-start.11 = (f32[128]{0:T(128)S(1)}, f32[128]{0:T(128)}, u32[]{:S(2)}) copy-start(f32[128]{0:T(128)} %param.29) | copy-start | bytes 1540
  3.0 11.8 %collective-permute-start = (bf16[14,4,16,128]{3,2,1,0:T(8,128)(2,1)S(1)}, bf16[14,4,16,128]{3,2,1,0:T(8,128)(2,1)S(1)}, u32[]{:S(2)}, u32[]{:S(2)}) collective-permute-start(bf16[14,4,16,128]{3,2,1,0:T(8,128)(2,1)S(1)} %fusion.2), channel_id=1, source_target_pairs={{0,32},{32,64},{64,96},{96,128},{128,160},{160,192},{192,224},{224... | collective-permute-start | bytes 688136 | tf_op jit(solution)/shard_map/ppermute | solution.py:291
  7.0 2.2 %copy-start.7 = (bf16[128,32]{0,1:T(8,128)(2,1)S(1)}, bf16[128,32]{0,1:T(8,128)(2,1)}, u32[]{:S(2)}) copy-start(bf16[128,32]{0,1:T(8,128)(2,1)} %param.28) | copy-start | bytes 24580
  7.0 2.3 %copy-start.9 = (f32[128]{0:T(128)S(1)}, f32[128]{0:T(128)}, u32[]{:S(2)}) copy-start(f32[128]{0:T(128)} %param.31) | copy-start | bytes 1540
  9.2 0.7 copy-start.12
  9.3 5.5 %copy-start.1 = (bf16[256,128]{1,0:T(8,128)(2,1)S(1)}, bf16[256,128]{1,0:T(8,128)(2,1)}, u32[]{:S(2)}) copy-start(bf16[256,128]{1,0:T(8,128)(2,1)} %wp_ref.1) | copy-start | bytes 196612
  9.3 5.5 %copy-start.2 = (s32[16,512]{1,0:T(8,128)S(1)}, s32[16,512]{1,0:T(8,128)}, u32[]{:S(2)}) copy-start(s32[16,512]{1,0:T(8,128)} %cnt_ref.1) | copy-start | bytes 98308
  10.2 40.8 %copy-start = (bf16[256,256]{1,0:T(8,128)(2,1)}, bf16[256,256]{1,0:T(8,128)(2,1)S(1)}, u32[]{:S(2)}) copy-start(bf16[256,256]{1,0:T(8,128)(2,1)S(1)} %fusion.perm_ref) | copy-start | bytes 393220
  51.1 8.5 %copy-start.4 = (bf16[128,128]{1,0:T(8,128)(2,1)S(1)}, bf16[128,128]{1,0:T(8,128)(2,1)}, u32[]{:S(2)}) copy-start(bf16[128,128]{1,0:T(8,128)(2,1)} %param.35) | copy-start | bytes 98308
  51.1 9.2 %copy-start.5 = (bf16[128,128]{1,0:T(8,128)(2,1)S(1)}, bf16[128,128]{1,0:T(8,128)(2,1)}, u32[]{:S(2)}) copy-start(bf16[128,128]{1,0:T(8,128)(2,1)} %param.34) | copy-start | bytes 98308
  51.1 9.2 %copy-start.6 = (bf16[128,128]{1,0:T(8,128)(2,1)S(1)}, bf16[128,128]{1,0:T(8,128)(2,1)}, u32[]{:S(2)}) copy-start(bf16[128,128]{1,0:T(8,128)(2,1)} %param.33) | copy-start | bytes 98308
  51.1 36.7 %all-to-all-start = ((bf16[32,16,16,128]{3,2,1,0:T(8,128)(2,1)}), bf16[32,16,16,128]{3,2,1,0:T(8,128)(2,1)S(1)}, u32[]{:S(2)}, u32[]{:S(2)}) async-start(bf16[32,16,16,128]{3,2,1,0:T(8,128)(2,1)} %pixel_pool.1), calls=%async_computation | async-start | bytes 4194304 | tf_op jit(solution)/shard_map/all_to_all | solution.py:300
  87.8 1.3 copy-start.3

commit v2 on v1

v2 whole, which is shorter than its diff:
```python
import functools
import math

import jax
import jax.numpy as jnp
from jax import lax
from jax.experimental import pallas as pl
from jax.experimental.pallas import tpu as pltpu
from jax.sharding import PartitionSpec as P

HEADS = 4
VAR_FLOOR = 0.05
NORM_EPS = 1e-05
F32 = jnp.float32
BF16 = jnp.bfloat16
LANES = 128


def three_parts(values):
    high = lax.reduce_precision(values, 8, 7)
    rest = values - high
    middle = lax.reduce_precision(rest, 8, 7)
    low = rest - middle
    return high.astype(BF16), middle.astype(BF16), low.astype(BF16)


def pixel_weights(w_first, b_first, w_second, b_second, dates):
    first = jnp.tile(jnp.concatenate([w_first.T, jnp.stack(three_parts(b_first))], axis=0), (1, dates))
    second = jnp.tile(w_second.T, (4, 4))
    bias = jnp.tile(jnp.stack(three_parts(b_second)), (1, 4))
    return first, second, bias


def relu_bf16(values):
    return jnp.maximum(values, 0.0).astype(BF16)


def spread_weights(t1_ref, t2_ref, b2_ref, w1_ref, w2_ref):
    taps, wide = t1_ref.shape
    groups = w2_ref.shape[0]
    dates = 4 * groups
    zero = jnp.zeros((), BF16)
    row = lax.broadcasted_iota(jnp.int32, (dates, wide), 0)
    col = lax.broadcasted_iota(jnp.int32, (dates, wide), 1)
    keep = row == col // (wide // dates)
    for b in range(taps):
        line = jnp.broadcast_to(t1_ref[b : b + 1, :].astype(F32), (dates, wide))
        w1_ref[b * dates : (b + 1) * dates, :] = jnp.where(keep, line, 0.0).astype(BF16)
    row_two = lax.broadcasted_iota(jnp.int32, (LANES, wide), 0)
    col_two = lax.broadcasted_iota(jnp.int32, (LANES, wide), 1)
    body = jnp.where(row_two // 32 == col_two // LANES, t2_ref[...].astype(F32), 0.0).astype(BF16)
    for g in range(groups):
        w2_ref[g, :LANES, :] = body
        w2_ref[g, LANES : 256 - 3 * dates, :] = jnp.zeros((LANES - 3 * dates, wide), BF16)
        mine = row == 4 * g + col // LANES
        for part in range(3):
            line = jnp.broadcast_to(b2_ref[part : part + 1, :].astype(F32), (dates, wide))
            start = 256 - 3 * dates + part * dates
            w2_ref[g, start : start + dates, :] = jnp.where(mine, line, 0.0).astype(BF16)


def swap_rows(size):
    row = lax.broadcasted_iota(jnp.int32, (size * size, size * size), 0)
    col = lax.broadcasted_iota(jnp.int32, (size * size, size * size), 1)
    return jnp.where(col == (row % size) * size + row // size, 1.0, 0.0).astype(BF16)


def pixel_kernel(
    pix_ref, cnt_ref, edge_ref, lot_ref, t1_ref, t2_ref, b2_ref, wp_ref, code_ref, out_ref,
    w1_ref, w2_ref, xt_ref, h_ref, es_ref, ec_ref, init_ref, inv_ref, pool_ref, e_ref, perm_ref, *, chunk,
):
    bands, slots, dates, lots = pix_ref.shape
    edge_slots = edge_ref.shape[1]
    groups = w2_ref.shape[0]
    block = pl.program_id(0)
    part_lots = LANES
    rows = part_lots // 4

    def mine(values):
        return jnp.concatenate([values[k + 8 * chunk : k + 8 * chunk + 8] for k in range(0, LANES, 16)], axis=0)

    def first_layer(count):
        def finish(r, z):
            z = relu_bf16(z)
            for g in range(4):
                h_ref[g, r, : count * rows, :] = z[:, g * LANES : (g + 1) * LANES]

        before = None
        for r in range(4):
            z = jnp.dot(xt_ref[r, : count * rows, :], w1_ref[...], preferred_element_type=F32)
            if before is not None:
                finish(r - 1, before)
            before = z
        finish(3, before)

    def hidden_two(g, r, count):
        a = jnp.concatenate([h_ref[g, r, : count * rows, :], xt_ref[r, : count * rows, LANES:]], axis=1)
        return jnp.dot(a, w2_ref[g], preferred_element_type=F32)

    def add_slots(z, count, lanes):
        total = square = None
        for p in range(count):
            part = jnp.maximum(z[p * rows : (p + 1) * rows, lanes], 0.0)
            total = part if total is None else total + part
            square = part * part if square is None else square + part * part
        return total, square

    @pl.when(block == 0)
    def _():
        spread_weights(t1_ref, t2_ref, b2_ref, w1_ref, w2_ref)
        perm_ref[...] = swap_rows(dates)
        half = LANES // 2
        ec = jnp.zeros((dates, LANES), F32)
        for p in range(edge_slots):
            mask = edge_ref[bands, p]
            xt = jnp.concatenate([edge_ref[b, p] for b in range(bands)] + [mask] * 3, axis=0).T
            for r in range(4):
                xt_ref[r, p * rows : (p + 1) * rows, :] = xt[r * rows : (r + 1) * rows]
            ec = ec + mask.astype(F32)
        ec_ref[...] = ec.astype(BF16)
        first_layer(edge_slots)
        es_ref[:, 3 * half :, :] = jnp.zeros((es_ref.shape[0], half, es_ref.shape[2]), BF16)

        @pl.loop(0, groups)
        def _(g):
            zs = [hidden_two(g, r, edge_slots) for r in range(4)]
            for c in range(2):
                lanes = slice(256 * c, 256 * (c + 1))
                stats = [add_slots(zs[r], edge_slots, lanes) for r in range(4)]
                for k in range(2):
                    for r in range(2):
                        v = stats[r][k] + stats[r + 2][k]
                        for part in range(3):
                            cut = v.astype(BF16)
                            here = slice(part * half + r * rows, part * half + (r + 1) * rows)
                            es_ref[2 * g + c, here, 256 * k : 256 * (k + 1)] = cut
                            v = v - cut.astype(F32)

    counts = cnt_ref[...]
    for p in range(slots):
        mask = jnp.where(counts > p, 1.0, 0.0).astype(BF16)
        for side in range(2):
            lanes = slice(side * LANES, (side + 1) * LANES)
            m = mask[:, lanes]
            x = jnp.concatenate([pix_ref[b, p, :, lanes] * m for b in range(bands)] + [m] * 3, axis=0)
            xt = mine(x.astype(F32).T).astype(BF16)
            for r in range(2):
                xt_ref[2 * side + r, p * rows : (p + 1) * rows, :] = xt[r * rows : (r + 1) * rows]
    first_layer(slots)

    lot = lot_ref[...]
    row = lax.broadcasted_iota(jnp.int32, (part_lots, 256), 0)
    lot_ids = block * lots + (row // 8) * 16 + 8 * chunk + row % 8
    chosen = jnp.where(lot_ids == lot, 1.0, 0.0).astype(BF16)
    lot_rows = lax.broadcasted_iota(jnp.int32, (lots, LANES), 0) + block * lots
    chosen_twice = jnp.where(lot_rows == lot[:, :LANES], 1.0, 0.0).astype(BF16)
    extra = lax.dot_general(ec_ref[...], chosen_twice, (((1,), (1,)), ((), ())), preferred_element_type=F32)
    inverse = 1.0 / (counts.astype(F32) + extra)
    inv_t = jnp.concatenate([mine(inverse[:, s * LANES : (s + 1) * LANES].T) for s in range(2)], axis=0)
    for d in range(dates):
        inv_ref[d] = jnp.broadcast_to(inv_t[:, d : d + 1], (part_lots, LANES))

    @pl.loop(0, groups)
    def _(g):
        def finish(r, z):
            here = slice(r * rows, (r + 1) * rows)
            for c in range(2):
                total, square = add_slots(z, slots, slice(256 * c, 256 * (c + 1)))
                total = total + init_ref[c, here, :256]
                square = square + init_ref[c, here, 256:]
                for k in range(2):
                    d = 4 * g + 2 * c + k
                    inv = inv_ref[d, here, :]
                    lanes = slice(k * LANES, (k + 1) * LANES)
                    average = total[:, lanes] * inv
                    spread = jnp.maximum(square[:, lanes] * inv - average * average, VAR_FLOOR)
                    spread = spread * lax.rsqrt(spread)
                    pool_ref[d, here, :LANES] = average.astype(BF16)
                    pool_ref[d, here, LANES:] = spread.astype(BF16)

        for c in range(2):
            init_ref[c] = jnp.dot(chosen, es_ref[2 * g + c], preferred_element_type=F32)
        before = None
        for r in range(4):
            z = hidden_two(g, r, slots)
            if before is not None:
                finish(r - 1, before)
            before = z
        finish(3, before)

    e_all = jnp.dot(pool_ref[...].reshape(dates * part_lots, 256), wp_ref[...], preferred_element_type=F32)
    for d in range(dates):
        e_ref[d] = (e_all[d * part_lots : (d + 1) * part_lots] + code_ref[d : d + 1, :]).astype(BF16)
    for k in range(0, part_lots, 32):
        both = jnp.concatenate(
            [e_ref[:, k + s : k + s + 16, :].reshape(dates * 16, LANES) for s in (0, 16)], axis=1
        )
        y = jnp.dot(perm_ref[...], both, preferred_element_type=F32).astype(BF16)
        for s in range(2):
            out_ref[k // 8 + 2 * s : k // 8 + 2 * s + 2] = y[:, s * LANES : (s + 1) * LANES].reshape(2, 8, dates, LANES)


def pool_lots(pixels, counts, edges, lots_owned, taps, w_pool, code, peers, chunk):
    bands, slots, dates, lots = pixels.shape
    own = lots // peers // 2
    block = 2 * LANES
    feats = w_pool.shape[1]
    groups = dates // 4
    whole = lambda x: pl.BlockSpec(x.shape, lambda i: (0,) * x.ndim, pipeline_mode=pl.Buffered(1))
    fixed = (edges, lots_owned, *taps, w_pool, code)
    return pl.pallas_call(
        functools.partial(pixel_kernel, chunk=chunk),
        grid=(lots // block,),
        in_specs=[
            pl.BlockSpec((bands, slots, dates, block), lambda i: (0, 0, 0, i)),
            pl.BlockSpec((dates, block), lambda i: (0, i)),
        ]
        + [whole(x) for x in fixed],
        out_specs=pl.BlockSpec((LANES // own, own, dates, feats), lambda i: (i, 0, 0, 0)),
        out_shape=jax.ShapeDtypeStruct((peers, own, dates, feats), BF16),
        scratch_shapes=[
            pltpu.VMEM((256, 512), BF16),
            pltpu.VMEM((groups, 256, 512), BF16),
            pltpu.VMEM((4, slots * LANES // 4, 256), BF16),
            pltpu.VMEM((4, 4, slots * LANES // 4, LANES), BF16),
            pltpu.VMEM((2 * groups, 256, 512), BF16),
            pltpu.VMEM((dates, LANES), BF16),
            pltpu.VMEM((2, LANES, 512), F32),
            pltpu.VMEM((dates, LANES, LANES), F32),
            pltpu.VMEM((dates, LANES, 256), BF16),
            pltpu.VMEM((dates, LANES, LANES), BF16),
            pltpu.VMEM((256, 256), BF16),
        ],
        compiler_params=pltpu.CompilerParams(vmem_limit_bytes=48 << 20),
        name=f"pixel_pool_{chunk}",
    )(pixels, counts, *fixed)


def erf_gelu(x):
    return 0.5 * x * (1.0 + lax.erf(x * (1.0 / math.sqrt(2.0))))


def norm_rows(x, gain):
    average = jnp.mean(x, axis=-1, keepdims=True)
    centered = x - average
    variance = jnp.mean(centered * centered, axis=-1, keepdims=True)
    return centered * lax.rsqrt(variance + NORM_EPS) * gain


def attention_kernel(
    e_ref, ln1_ref, wqv_ref, wkt_ref, wo_ref, ln2_ref, up_ref, down_ref, *rest, last,
):
    if last:
        first_ref, out_ref, enc_ref, q_ref, v_ref, k_ref, mix_ref = rest
    else:
        enc_ref, q_ref, v_ref, k_ref, mix_ref = rest
    peers, own, dates, width = e_ref.shape
    total = peers * dates
    head = width // HEADS
    together = q_ref.shape[0]
    tall = 256
    scale = math.log2(math.e) / math.sqrt(head)

    def rows_of(lot):
        return jnp.concatenate([e_ref[:, lot + l].reshape(total, width) for l in range(together)], axis=0).astype(F32)

    def project(lot):
        normed = norm_rows(rows_of(lot), ln1_ref[...]).astype(BF16)
        both = jnp.dot(normed, wqv_ref[...], preferred_element_type=F32).astype(BF16)
        keys_t = lax.dot_general(
            wkt_ref[...], normed, (((1,), (1,)), ((), ())), preferred_element_type=F32
        ).astype(BF16)
        for l in range(together):
            here = slice(l * total, (l + 1) * total)
            q_ref[l] = both[here, :width]
            v_ref[l] = both[here, width:]
            k_ref[l] = keys_t[:, here]

    def mix_dates(l):
        lane = lax.broadcasted_iota(jnp.int32, (total, width), 1)
        ones = jnp.ones((total, width), BF16)
        zero = jnp.zeros((total, width), BF16)
        parts = [None] * (total // tall)
        for h in range(HEADS):
            mine = lane // head == h
            queries = jnp.where(mine, q_ref[l], zero)
            values = jnp.concatenate([jnp.where(mine, v_ref[l], zero), ones], axis=1)
            for b in range(total // tall):
                here = slice(b * tall, (b + 1) * tall)
                scores = jnp.dot(queries[here], k_ref[l], preferred_element_type=F32)
                top = jnp.max(scores, axis=1, keepdims=True) * scale
                weights = jnp.exp2(scores * scale - top).astype(BF16)
                mix = jnp.dot(weights, values, preferred_element_type=F32)
                mix = mix[:, :width] * (1.0 / mix[:, width:])
                parts[b] = mix if parts[b] is None else parts[b] + mix
        mix_ref[l] = jnp.concatenate(parts, axis=0).astype(BF16)

    def feed_forward(lot):
        mixture = mix_ref[...].reshape(together * total, width)
        carried = rows_of(lot) + jnp.dot(mixture, wo_ref[...], preferred_element_type=F32)
        normed_two = norm_rows(carried, ln2_ref[...]).astype(BF16)
        hidden = erf_gelu(jnp.dot(normed_two, up_ref[...], preferred_element_type=F32)).astype(BF16)
        encoded = (carried + jnp.dot(hidden, down_ref[...], preferred_element_type=F32)).astype(BF16)
        for l in range(together):
            enc_ref[lot + l] = encoded[l * total : (l + 1) * total].reshape(peers, dates, width)

    @pl.loop(0, own, step=together)
    def _(lot):
        project(lot)

        @pl.loop(0, together, step=2)
        def _(l):
            mix_dates(l)
            mix_dates(l + 1)

        feed_forward(lot)

    if last:
        perm = swap_rows(dates)
        for p in range(0, peers, 2):
            two = jnp.concatenate(
                [
                    jnp.concatenate([first_ref[:, p + s], enc_ref[:, p + s]], axis=0).reshape(2 * own * dates, width)
                    for s in range(2)
                ],
                axis=1,
            )
            y = jnp.dot(perm, two, preferred_element_type=F32).astype(BF16)
            for s in range(2):
                here = slice((p + s) * dates, (p + s + 1) * dates)
                out_ref[here] = y[:, s * width : (s + 1) * width].reshape(dates, 2 * own, width)


def attend(embedded, params, first=None):
    peers, own, dates, width = embedded.shape
    total = peers * dates
    together = 4
    scratch = [
        pltpu.VMEM((together, total, width), BF16),
        pltpu.VMEM((together, total, width), BF16),
        pltpu.VMEM((together, width, total), BF16),
        pltpu.VMEM((together, total, width), BF16),
    ]
    last = first is not None
    mid = (own, peers, dates, width)
    return pl.pallas_call(
        functools.partial(attention_kernel, last=last),
        out_shape=jax.ShapeDtypeStruct((total, 2 * own, width) if last else mid, BF16),
        scratch_shapes=([pltpu.VMEM(mid, BF16)] if last else []) + scratch,
        compiler_params=pltpu.CompilerParams(vmem_limit_bytes=48 << 20),
        name="attend_last" if last else "attend_first",
    )(embedded, *params, *([first] if last else []))


def position_code(day_numbers, model_width):
    half_ids = jnp.arange(model_width // 2, dtype=F32)
    freq_rate = jnp.exp(-(2.0 * half_ids / model_width) * math.log(1000.0))
    phase_angle = day_numbers.astype(F32)[:, None] * freq_rate[None]
    return jnp.stack([jnp.sin(phase_angle), jnp.cos(phase_angle)], axis=-1).reshape(
        day_numbers.shape[0], model_width
    )


def edge_kernel(pix_ref, mask_ref, out_ref):
    bands, slots = pix_ref.shape[:2]
    half = slots // 2
    for p in range(half):
        masks = [jnp.where(mask_ref[p + s * half] > 0, 1.0, 0.0) for s in range(2)]
        out_ref[bands, p] = jnp.concatenate(masks, axis=-1).astype(BF16)
        for b in range(bands):
            two = [pix_ref[b, p + s * half].astype(F32) * masks[s] for s in range(2)]
            out_ref[b, p] = jnp.concatenate(two, axis=-1).astype(BF16)


def edge_rows(edge_pixels, edge_mask):
    bands, slots, dates, blocks = edge_pixels.shape
    return pl.pallas_call(
        edge_kernel,
        out_shape=jax.ShapeDtypeStruct((bands + 1, slots // 2, dates, 2 * blocks), BF16),
        name="edge_rows",
    )(edge_pixels, edge_mask)


def per_device(
    pixels, counts, edge_pixels, edge_mask, straddle_lot, date_days,
    w_first, b_first, w_second, b_second, w_pool, b_pool,
    ln_one, w_query, w_key, w_value, w_out, ln_two, w_up, w_down,
):
    groups = lax.axis_size("group")
    peers = lax.axis_size("date")
    dates = pixels.shape[2]
    width = w_pool.shape[1]
    edges = lax.ppermute(
        edge_rows(edge_pixels, edge_mask), "group", [(i, (i + 1) % groups) for i in range(groups)]
    )
    taps = pixel_weights(w_first, b_first, w_second, b_second, dates)
    own_days = lax.dynamic_slice_in_dim(date_days, lax.axis_index("date") * dates, dates)
    code = position_code(own_days, width) + b_pool
    lots_owned = jnp.concatenate([straddle_lot] * 3 + [jnp.full_like(straddle_lot, -1)])[None]
    params = (
        ln_one[None], jnp.concatenate([w_query, w_value], axis=1), w_key.T, w_out, ln_two[None], w_up, w_down
    )
    series = []
    for chunk in range(2):
        pooled = pool_lots(pixels, counts, edges, lots_owned, taps, w_pool, code, peers, chunk)
        series.append(lax.all_to_all(pooled, "date", split_axis=0, concat_axis=0, tiled=True))
    return attend(series[1], params, attend(series[0], params))


def solution(mesh):
    return jax.shard_map(
        per_device,
        mesh=mesh,
        in_specs=(
            P(None, None, "date", "group"),
            P("date", "group"),
            P(None, None, "date", "group"),
            P(None, "date", "group"),
            P("group"),
        )
        + (P(),) * 15,
        out_specs=P(None, ("group", "date"), None),
        check_vma=False,
    )
```

time: 149 us -> 111 us (0.74)
  waiting for transfers between devices: 31.5 us -> 3.94 us
  Pallas kernels: 95.8 us -> 80.7 us
  starting transfers between devices: 11 us -> 18.3 us
  local copies, waits for them, and re-layouts: 4.48 us -> 2.84 us
    all_to_all x1 -> x2, waiting for transfers between devices: 26.9 us -> 0.01 us  [per_device(): lax.all_to_all(pooled, 'date', split_axis=0, concat_axis=0, tiled=True)]
    pallas_call x2 -> x5, Pallas kernels: 95.8 us -> 80.7 us  [the longest x2 40.7 us: pool_lots(): pl.pallas_call(functools.partial(pixel_kernel, chunk=chunk), grid=(lots /...]
    all_to_all x1 -> x2, starting transfers between devices: 8.43 us -> 15.8 us  [per_device(): lax.all_to_all(pooled, 'date', split_axis=0, concat_axis=0, tiled=True)]
    mul x8 -> x0, local copies, waits for them, and re-layouts: 2.03 us -> none  [the longest x1 0.78 us: pixel_weights(): w_first.T[:, None, None, :] * same[None, :, :, None]]
  transfers between devices with their start and end apart: 2 -> 3, of which waited for: 2 -> 1; matrix products, arithmetic and copies ran while one was open for 4% -> 5% of each run, Pallas kernels for 0% -> 35%
where the time goes in v2:
time: 111 us; the launch traced here: 110 us
  Pallas kernels  80.7 us (73%)
  starting transfers between devices  18.3 us (16%)
  other arithmetic  4.44 us (4%)
  waiting for transfers between devices  3.94 us (4%)
  local copies, waits for them, and re-layouts  2.84 us (3%)
    pallas_call x2, Pallas kernels, pool_lots(): pl.pallas_call(functools.partial(pixel_kernel, chunk=chunk), grid=(lots /...  40.7 us
    pallas_call x2, Pallas kernels, attend(): pl.pallas_call(functools.partial(attention_kernel, last=last), out_shape=...  38.1 us
    all_to_all x2, starting transfers between devices, per_device(): lax.all_to_all(pooled, 'date', split_axis=0, concat_axis=0, tiled=True)  15.8 us
    ppermute x1, waiting for transfers between devices, per_device(): lax.ppermute(edge_rows(edge_pixels, edge_mask), 'group', [(i, (i + 1) % g...  3.93 us
    ppermute x1, starting transfers between devices, per_device(): lax.ppermute(edge_rows(edge_pixels, edge_mask), 'group', [(i, (i + 1) % g...  2.47 us
  transfers between devices with their start and end apart: 3, of which 1 were waited for; matrix products, arithmetic and copies ran while one was open for 5% of the time, Pallas kernels for 35%

profile of v2, /device:TPU:1, one launch (start us, length us, event | category | flops | bytes accessed | tf_op | source)
XLA Modules:
  0.0 110.4 jit_solution(9352765865078132625)
XLA Ops:
  0.0 1.9 %edge_rows.1 = bf16[14,4,16,128]{3,2,1,0:T(8,128)(2,1)} custom-call(bf16[13,8,16,64]{3,2,1,0:T(8,128)(2,1)} %pix_ref.3, s32[8,16,64]{2,1,0:T(8,128)} %mask_ref.1), custom_call_target="tpu_custom_call" | custom-call | tf_op jit(solution)/shard_map/edge_rows/pallas_call | solution.py:377
  1.9 2.5 %collective-permute-start = (bf16[14,4,16,128]{3,2,1,0:T(8,128)(2,1)}, bf16[14,4,16,128]{3,2,1,0:T(8,128)(2,1)S(1)}, u32[]{:S(2)}, u32[]{:S(2)}) collective-permute-start(bf16[14,4,16,128]{3,2,1,0:T(8,128)(2,1)} %edge_rows.1), channel_id=1, source_target_pairs={{0,32},{32,64},{64,96},{96,128},{128,160},{160,192},{192,224},{224... | collective-permute-start | bytes 688136 | tf_op jit(solution)/shard_map/ppermute | solution.py:393
  4.3 0.7 fusion
  5.0 0.7 fusion.4
  5.7 0.8 dynamic-slice_convert_fusion
  6.5 0.1 multiply_sine_fusion
  6.6 0.7 pad_maximum_fusion.1
  7.3 0.8 pad_add_fusion
  8.1 0.1 copy.24
  8.2 0.1 copy.25
  8.3 0.1 tile.13.t1_ref
  8.4 0.7 tile.14
  9.2 0.7 broadcast_add_fusion.code_ref
  9.9 3.9 %collective-permute-done.edge_ref = bf16[14,4,16,128]{3,2,1,0:T(8,128)(2,1)S(1)} collective-permute-done((bf16[14,4,16,128]{3,2,1,0:T(8,128)(2,1)}, bf16[14,4,16,128]{3,2,1,0:T(8,128)(2,1)S(1)}, u32[]{:S(2)}, u32[]{:S(2)}) %collective-permute-start) | collective-permute-done | bytes 229408 | tf_op jit(solution)/shard_map/ppermute | solution.py:393
  13.8 0.8 copy-done.2
  14.7 0.8 copy-done.4
  15.4 20.4 %pixel_pool_0.1 = bf16[32,8,16,128]{3,2,1,0:T(8,128)(2,1)} custom-call(bf16[13,24,16,512]{3,2,1,0:T(8,128)(2,1)} %pix_ref.5, s32[16,512]{1,0:T(8,128)S(1)} %copy-done.4, bf16[14,4,16,128]{3,2,1,0:T(8,128)(2,1)S(1)} %collective-permute-done.edge_ref, s32[1,256]{1,0:T(1,128)S(1)} %bitcast.35, bf16[16,512]{1,0:T(8,128)(2,1)S(1)} %tile.13.t1_ref, ...), custom_call_target="tpu_custom_call" | custom-call | tf_op jit(solution)/shard_map/pixel_pool_0/pallas_call | solution.py:211
  35.8 0.0 copy-start.6
  35.8 8.5 %all-to-all-start.1 = ((bf16[32,8,16,128]{3,2,1,0:T(8,128)(2,1)}), bf16[32,8,16,128]{3,2,1,0:T(8,128)(2,1)S(1)}, u32[]{:S(2)}, u32[]{:S(2)}) async-start(bf16[32,8,16,128]{3,2,1,0:T(8,128)(2,1)} %pixel_pool_0.1), calls=%async_computation.1 | async-start | bytes 2097152 | tf_op jit(solution)/shard_map/all_to_all | solution.py:406
  44.3 20.3 %pixel_pool_1.1 = bf16[32,8,16,128]{3,2,1,0:T(8,128)(2,1)} custom-call(bf16[13,24,16,512]{3,2,1,0:T(8,128)(2,1)} %pix_ref.5, s32[16,512]{1,0:T(8,128)S(1)} %copy-done.5, bf16[14,4,16,128]{3,2,1,0:T(8,128)(2,1)S(1)} %collective-permute-done.edge_ref, s32[1,256]{1,0:T(1,128)S(1)} %bitcast.36, bf16[16,512]{1,0:T(8,128)(2,1)S(1)} %tile.13.t1_ref, ...), custom_call_target="tpu_custom_call" | custom-call | tf_op jit(solution)/shard_map/pixel_pool_1/pallas_call | solution.py:211
  64.7 7.4 %all-to-all-start = ((bf16[32,8,16,128]{3,2,1,0:T(8,128)(2,1)}), bf16[32,8,16,128]{3,2,1,0:T(8,128)(2,1)S(1)}, u32[]{:S(2)}, u32[]{:S(2)}) async-start(bf16[32,8,16,128]{3,2,1,0:T(8,128)(2,1)} %pixel_pool_1.1), calls=%async_computation | async-start | bytes 2097152 | tf_op jit(solution)/shard_map/all_to_all | solution.py:406
  72.1 0.1 copy.26
  72.3 18.0 %attend_first.1.rest_0_ = bf16[8,32,16,128]{3,2,1,0:T(8,128)(2,1)S(1)} custom-call(bf16[32,8,16,128]{3,2,1,0:T(8,128)(2,1)S(1)} %all-to-all-done.1.e_ref, f32[1,128]{1,0:T(1,128)S(1)} %bitcast.37, bf16[128,256]{1,0:T(8,128)(2,1)S(1)} %constant_dynamic-update-slice_fusion.wqv_ref, bf16[128,128]{1,0:T(8,128)(2,1)S(1)} %bitcast.31, ...), custom_call_target="tpu_custom_call" | custom-call | tf_op jit(solution)/shard_map/attend_first/pallas_call | solution.py:346
  90.3 20.1 %attend_last.1 = bf16[512,16,128]{2,1,0:T(8,128)(2,1)} custom-call(bf16[32,8,16,128]{3,2,1,0:T(8,128)(2,1)S(1)} %all-to-all-done.e_ref, f32[1,128]{1,0:T(1,128)S(1)} %bitcast.38, bf16[128,256]{1,0:T(8,128)(2,1)S(1)} %constant_dynamic-update-slice_fusion.wqv_ref, bf16[128,128]{1,0:T(8,128)(2,1)S(1)} %bitcast.32, bf16[128,128]{1,0:T(8,128)(2,1)S(1)} %copy-done.6, ...), custom_call_target="tpu_custom_call" | custom-call | tf_op jit(solution)/shard_map/attend_last/pallas_call | solution.py:346
  (33 shorter events, 0.2 us)
Async XLA Ops:
  0.0 44.3 %copy-start.3 = (bf16[256,128]{1,0:T(8,128)(2,1)S(1)}, bf16[256,128]{1,0:T(8,128)(2,1)}, u32[]{:S(2)}) copy-start(bf16[256,128]{1,0:T(8,128)(2,1)} %wp_ref.3) | copy-start | bytes 196612
  0.0 44.3 %copy-start.5 = (s32[16,512]{1,0:T(8,128)S(1)}, s32[16,512]{1,0:T(8,128)}, u32[]{:S(2)}) copy-start(s32[16,512]{1,0:T(8,128)} %cnt_ref.3) | copy-start | bytes 98308
  1.9 11.9 %collective-permute-start = (bf16[14,4,16,128]{3,2,1,0:T(8,128)(2,1)}, bf16[14,4,16,128]{3,2,1,0:T(8,128)(2,1)S(1)}, u32[]{:S(2)}, u32[]{:S(2)}) collective-permute-start(bf16[14,4,16,128]{3,2,1,0:T(8,128)(2,1)} %edge_rows.1), channel_id=1, source_target_pairs={{0,32},{32,64},{64,96},{96,128},{128,160},{160,192},{192,224},{224... | collective-permute-start | bytes 688136 | tf_op jit(solution)/shard_map/ppermute | solution.py:393
  13.8 0.8 copy-start.2
  14.6 0.8 copy-start.4
  35.8 36.3 %copy-start.9 = (bf16[128,128]{1,0:T(8,128)(2,1)S(1)}, bf16[128,128]{1,0:T(8,128)(2,1)}, u32[]{:S(2)}) copy-start(bf16[128,128]{1,0:T(8,128)(2,1)} %param.34) | copy-start | bytes 98308
  35.8 36.4 %copy-start.10 = (bf16[128,128]{1,0:T(8,128)(2,1)S(1)}, bf16[128,128]{1,0:T(8,128)(2,1)}, u32[]{:S(2)}) copy-start(bf16[128,128]{1,0:T(8,128)(2,1)} %param.33) | copy-start | bytes 98308
  35.8 36.4 %copy-start.11 = (bf16[128,128]{1,0:T(8,128)(2,1)S(1)}, bf16[128,128]{1,0:T(8,128)(2,1)}, u32[]{:S(2)}) copy-start(bf16[128,128]{1,0:T(8,128)(2,1)} %param.35) | copy-start | bytes 98308
  35.8 36.4 %copy-start = (bf16[128,512]{1,0:T(8,128)(2,1)S(1)}, bf16[128,512]{1,0:T(8,128)(2,1)}, u32[]{:S(2)}) copy-start(bf16[128,512]{1,0:T(8,128)(2,1)} %up_ref.3) | copy-start | bytes 393220
  35.8 36.4 %copy-start.1 = (bf16[512,128]{1,0:T(8,128)(2,1)S(1)}, bf16[512,128]{1,0:T(8,128)(2,1)}, u32[]{:S(2)}) copy-start(bf16[512,128]{1,0:T(8,128)(2,1)} %down_ref.3) | copy-start | bytes 393220
  35.8 36.4 %copy-start.6 = (bf16[128,128]{1,0:T(8,128)(2,1)S(1)}, bf16[128,128]{1,0:T(8,128)(2,1)}, u32[]{:S(2)}) copy-start(bf16[128,128]{1,0:T(8,128)(2,1)} %wo_ref.3) | copy-start | bytes 98308
  35.8 36.4 %copy-start.7 = (f32[128]{0:T(128)S(1)}, f32[128]{0:T(128)}, u32[]{:S(2)}) copy-start(f32[128]{0:T(128)} %param.32) | copy-start | bytes 1540
  35.8 36.4 %copy-start.8 = (f32[128]{0:T(128)S(1)}, f32[128]{0:T(128)}, u32[]{:S(2)}) copy-start(f32[128]{0:T(128)} %param.37) | copy-start | bytes 1540
  35.8 28.8 %all-to-all-start.1 = ((bf16[32,8,16,128]{3,2,1,0:T(8,128)(2,1)}), bf16[32,8,16,128]{3,2,1,0:T(8,128)(2,1)S(1)}, u32[]{:S(2)}, u32[]{:S(2)}) async-start(bf16[32,8,16,128]{3,2,1,0:T(8,128)(2,1)} %pixel_pool_0.1), calls=%async_computation.1 | async-start | bytes 2097152 | tf_op jit(solution)/shard_map/all_to_all | solution.py:406
  64.7 25.7 %all-to-all-start = ((bf16[32,8,16,128]{3,2,1,0:T(8,128)(2,1)}), bf16[32,8,16,128]{3,2,1,0:T(8,128)(2,1)S(1)}, u32[]{:S(2)}, u32[]{:S(2)}) async-start(bf16[32,8,16,128]{3,2,1,0:T(8,128)(2,1)} %pixel_pool_1.1), calls=%async_computation | async-start | bytes 2097152 | tf_op jit(solution)/shard_map/all_to_all | solution.py:406

commit v3 on v2

v3 whole, which is shorter than its diff:
```python
import functools
import math

import jax
import jax.numpy as jnp
from jax import lax
from jax.experimental import pallas as pl
from jax.experimental.pallas import tpu as pltpu
from jax.sharding import PartitionSpec as P

HEADS = 4
VAR_FLOOR = 0.05
NORM_EPS = 1e-05
F32 = jnp.float32
BF16 = jnp.bfloat16
LANES = 128


def relu_bf16(values):
    return jnp.maximum(values, 0.0).astype(BF16)


NT = (((1,), (1,)), ((), ()))


def ones_where(condition):
    return jnp.where(condition, 1.0, 0.0).astype(BF16)


def grid_of(shape):
    return lax.broadcasted_iota(jnp.int32, shape, 0), lax.broadcasted_iota(jnp.int32, shape, 1)


def three_parts(values):
    parts = []
    for _ in range(3):
        parts.append(values.astype(BF16))
        values = values - parts[-1].astype(F32)
    return parts


def spread_weights(wf_ref, bf_ref, ws_ref, bs_ref, w1_ref, w2_ref):
    h1, bands = wf_ref.shape
    feats = ws_ref.shape[0]
    groups = w2_ref.shape[0]
    dates = 4 * groups
    wide = dates * h1
    row, col = grid_of((h1, wide))
    repeat = ones_where(row == col % h1)
    row, col = grid_of((16, bands))
    turned = lax.dot_general(ones_where(row == col), wf_ref[...], NT, preferred_element_type=F32).astype(BF16)
    taps = jnp.dot(turned, repeat, preferred_element_type=F32)
    row, col = grid_of((dates, wide))
    keep = row == col // h1
    for b in range(bands):
        line = jnp.broadcast_to(taps[b : b + 1], (dates, wide))
        w1_ref[b * dates : (b + 1) * dates, :] = jnp.where(keep, line, 0.0).astype(BF16)
    for part, values in enumerate(three_parts(jnp.broadcast_to(bf_ref[...], (dates, h1)))):
        line = jnp.dot(values, repeat, preferred_element_type=F32)
        start = (bands + part) * dates
        w1_ref[start : start + dates, :] = jnp.where(keep, line, 0.0).astype(BF16)
    row, col = grid_of((4 * h1, h1))
    stacked = lax.dot_general(ones_where(row % h1 == col), ws_ref[...], NT, preferred_element_type=F32)
    row_two, col_two = grid_of((4 * h1, 4 * feats))
    body = jnp.where(row_two // h1 == col_two // feats, jnp.concatenate([stacked] * 4, axis=1), 0.0).astype(BF16)
    lines = [part.astype(F32) for part in three_parts(jnp.broadcast_to(bs_ref[...], (dates, feats)))]
    lines = [jnp.concatenate([line] * 4, axis=1) for line in lines]
    row, col = grid_of((dates, 4 * feats))
    gap = 256 - 3 * dates
    for g in range(groups):
        w2_ref[g, : 4 * h1, :] = body
        w2_ref[g, 4 * h1 : gap, :] = jnp.zeros((gap - 4 * h1, 4 * feats), BF16)
        for part in range(3):
            start = gap + part * dates
            w2_ref[g, start : start + dates, :] = jnp.where(row == 4 * g + col // feats, lines[part], 0.0).astype(BF16)


def swap_rows(size):
    row = lax.broadcasted_iota(jnp.int32, (size * size, size * size), 0)
    col = lax.broadcasted_iota(jnp.int32, (size * size, size * size), 1)
    return jnp.where(col == (row % size) * size + row // size, 1.0, 0.0).astype(BF16)


ROWS = 32


def first_layer(xt, h_ref, w1_ref, count):
    def finish(r, z):
        z = relu_bf16(z)
        for g in range(4):
            h_ref[g, r, : count * ROWS, :] = z[:, g * LANES : (g + 1) * LANES]

    before = None
    for r in range(4):
        z = jnp.dot(xt(r), w1_ref[...], preferred_element_type=F32)
        if before is not None:
            finish(r - 1, before)
        before = z
    finish(3, before)


def second_layer(xt, h_ref, w2_ref, g, r, count):
    a = jnp.concatenate([h_ref[g, r, : count * ROWS, :], xt(r)[:, LANES:]], axis=1)
    return jnp.dot(a, w2_ref[g], preferred_element_type=F32)


def add_slots(z, count, lanes):
    total = square = None
    for p in range(count):
        part = jnp.maximum(z[p * ROWS : (p + 1) * ROWS, lanes], 0.0)
        total = part if total is None else total + part
        square = part * part if square is None else square + part * part
    return total, square


def halves(values):
    return [
        jnp.concatenate([values[k + 8 * c : k + 8 * c + 8] for k in range(0, LANES, 16)], axis=0) for c in range(2)
    ]


def sums_of(xt, h_ref, w1_ref, w2_ref, out_ref, slots):
    first_layer(xt, h_ref, w1_ref, slots)

    @pl.loop(0, w2_ref.shape[0])
    def _(g):
        def finish(r, z):
            here = slice(r * ROWS, (r + 1) * ROWS)
            for c in range(2):
                total, square = add_slots(z, slots, slice(256 * c, 256 * (c + 1)))
                out_ref[0, g, c, here, :256] = total
                out_ref[0, g, c, here, 256:] = square

        before = None
        for r in range(4):
            z = second_layer(xt, h_ref, w2_ref, g, r, slots)
            if before is not None:
                finish(r - 1, before)
            before = z
        finish(3, before)


def first_sums_kernel(
    pix_ref, cnt_ref, wf_ref, bf_ref, ws_ref, bs_ref, out_ref, other_ref, w1_ref, w2_ref, xt_ref, h_ref
):
    bands, slots = pix_ref.shape[:2]

    @pl.when(pl.program_id(0) == 0)
    def _():
        spread_weights(wf_ref, bf_ref, ws_ref, bs_ref, w1_ref, w2_ref)

    counts = cnt_ref[...]
    for p in range(slots):
        mask = ones_where(counts > p)
        for side in range(2):
            lanes = slice(side * LANES, (side + 1) * LANES)
            m = mask[:, lanes]
            x = jnp.concatenate([pix_ref[b, p, :, lanes] * m for b in range(bands)] + [m] * 3, axis=0)
            for c, xt in enumerate(halves(x.astype(F32).T)):
                xt = xt.astype(BF16)
                for r in range(2):
                    part = xt[r * ROWS : (r + 1) * ROWS]
                    if c == 0:
                        xt_ref[2 * side + r, p * ROWS : (p + 1) * ROWS, :] = part
                    else:
                        other_ref[0, 2 * side + r, p * ROWS : (p + 1) * ROWS, :] = part
    sums_of(lambda r: xt_ref[r], h_ref, w1_ref, w2_ref, out_ref, slots)


def second_sums_kernel(xt_ref, wf_ref, bf_ref, ws_ref, bs_ref, out_ref, w1_ref, w2_ref, h_ref):
    @pl.when(pl.program_id(0) == 0)
    def _():
        spread_weights(wf_ref, bf_ref, ws_ref, bs_ref, w1_ref, w2_ref)

    sums_of(lambda r: xt_ref[0, r], h_ref, w1_ref, w2_ref, out_ref, xt_ref.shape[2] // ROWS)


def edge_sums_kernel(edge_ref, wf_ref, bf_ref, ws_ref, bs_ref, es_ref, ec_ref, w1_ref, w2_ref, xt_ref, h_ref):
    bands = edge_ref.shape[0] - 1
    slots, dates = edge_ref.shape[1:3]
    half = LANES // 2
    spread_weights(wf_ref, bf_ref, ws_ref, bs_ref, w1_ref, w2_ref)
    ec = jnp.zeros((dates, LANES), F32)
    for p in range(slots):
        mask = edge_ref[bands, p]
        xt = jnp.concatenate([edge_ref[b, p] for b in range(bands)] + [mask] * 3, axis=0).T
        for r in range(4):
            xt_ref[r, p * ROWS : (p + 1) * ROWS, :] = xt[r * ROWS : (r + 1) * ROWS]
        ec = ec + mask.astype(F32)
    ec_ref[...] = ec.astype(BF16)
    first_layer(lambda r: xt_ref[r], h_ref, w1_ref, slots)
    es_ref[:, 3 * half :, :] = jnp.zeros((es_ref.shape[0], half, es_ref.shape[2]), BF16)

    @pl.loop(0, w2_ref.shape[0])
    def _(g):
        zs = [second_layer(lambda r: xt_ref[r], h_ref, w2_ref, g, r, slots) for r in range(4)]
        for c in range(2):
            lanes = slice(256 * c, 256 * (c + 1))
            stats = [add_slots(zs[r], slots, lanes) for r in range(4)]
            for k in range(2):
                for r in range(2):
                    v = stats[r][k] + stats[r + 2][k]
                    for part, cut in enumerate(three_parts(v)):
                        here = slice(part * half + r * ROWS, part * half + (r + 1) * ROWS)
                        es_ref[2 * g + c, here, 256 * k : 256 * (k + 1)] = cut


def pool_kernel(
    sums_ref, cnt_ref, es_ref, ec_ref, lot_ref, wp_ref, code_ref, out_ref,
    chosen_ref, inv_ref, pool_ref, e_ref, perm_ref, *, chunk,
):
    block, g = pl.program_id(0), pl.program_id(1)
    dates, lots = cnt_ref.shape

    @pl.when(g == 0)
    def _():
        perm_ref[...] = swap_rows(dates)
        lot = jnp.concatenate([lot_ref[...], lot_ref[...]], axis=1)
        lane = lax.broadcasted_iota(jnp.int32, lot.shape, 1)
        four = jnp.concatenate([lot, jnp.where(lane < LANES // 2, lot, -1)], axis=1)
        row = lax.broadcasted_iota(jnp.int32, (LANES, 256), 0)
        lot_ids = block * lots + (row // 8) * 16 + 8 * chunk + row % 8
        chosen_ref[...] = ones_where(lot_ids == four)
        lot_rows = lax.broadcasted_iota(jnp.int32, (lots, LANES), 0) + block * lots
        extra = lax.dot_general(ec_ref[...], ones_where(lot_rows == lot), NT, preferred_element_type=F32)
        inverse = 1.0 / (cnt_ref[...].astype(F32) + extra)
        inv_t = jnp.concatenate(
            [halves(inverse[:, s * LANES : (s + 1) * LANES].T)[chunk] for s in range(2)], axis=0
        )
        for d in range(dates):
            inv_ref[d] = jnp.broadcast_to(inv_t[:, d : d + 1], (LANES, LANES))

    for c in range(2):
        both = sums_ref[0, 0, c] + jnp.dot(chosen_ref[...], es_ref[c], preferred_element_type=F32)
        for k in range(2):
            d = 4 * g + 2 * c + k
            inv = inv_ref[d]
            average = both[:, k * LANES : (k + 1) * LANES] * inv
            spread = both[:, (2 + k) * LANES : (3 + k) * LANES] * inv - average * average
            spread = jnp.maximum(spread, VAR_FLOOR)
            spread = spread * lax.rsqrt(spread)
            pool_ref[d, :, :LANES] = average.astype(BF16)
            pool_ref[d, :, LANES:] = spread.astype(BF16)

    @pl.when(g == pl.num_programs(1) - 1)
    def _():
        e_all = jnp.dot(pool_ref[...].reshape(dates * LANES, 256), wp_ref[...], preferred_element_type=F32)
        for d in range(dates):
            e_ref[d] = (e_all[d * LANES : (d + 1) * LANES] + code_ref[d : d + 1, :]).astype(BF16)
        for k in range(0, LANES, 32):
            both = jnp.concatenate(
                [e_ref[:, k + s : k + s + 16, :].reshape(dates * 16, LANES) for s in (0, 16)], axis=1
            )
            y = jnp.dot(perm_ref[...], both, preferred_element_type=F32).astype(BF16)
            for s in range(2):
                here = slice(k // 8 + 2 * s, k // 8 + 2 * s + 2)
                out_ref[here] = y[:, s * LANES : (s + 1) * LANES].reshape(2, 8, dates, LANES)


def whole(x):
    return pl.BlockSpec(x.shape, lambda *_: (0,) * x.ndim, pipeline_mode=pl.Buffered(1))


def own_sums(weights, slots, dates, blocks, pixels=None, counts=None, turned=None):
    groups = dates // 4
    sums = jax.ShapeDtypeStruct((blocks, groups, 2, LANES, 512), F32)
    sums_spec = pl.BlockSpec((1,) + sums.shape[1:], lambda i: (i, 0, 0, 0, 0))
    tall = slots * ROWS
    laid = jax.ShapeDtypeStruct((blocks, 4, tall, 256), BF16)
    laid_spec = pl.BlockSpec((1,) + laid.shape[1:], lambda i: (i, 0, 0, 0))
    scratch = [pltpu.VMEM((256, 512), BF16), pltpu.VMEM((groups, 256, 512), BF16)]
    hidden = pltpu.VMEM((4, 4, tall, LANES), BF16)
    first = turned is None
    if first:
        bands = pixels.shape[0]
        inputs = (pixels, counts)
        specs = [
            pl.BlockSpec((bands, slots, dates, 256), lambda i: (0, 0, 0, i)),
            pl.BlockSpec((dates, 256), lambda i: (0, i)),
        ]
        scratch.append(pltpu.VMEM((4, tall, 256), BF16))
    else:
        inputs, specs = (turned,), [laid_spec]
    return pl.pallas_call(
        first_sums_kernel if first else second_sums_kernel,
        grid=(blocks,),
        in_specs=specs + [whole(x) for x in weights],
        out_specs=(sums_spec, laid_spec) if first else sums_spec,
        out_shape=(sums, laid) if first else sums,
        scratch_shapes=scratch + [hidden],
        compiler_params=pltpu.CompilerParams(vmem_limit_bytes=58 << 20),
        name="first_sums" if first else "second_sums",
    )(*inputs, *weights)


def edge_sums(edges, weights):
    _, slots, dates, lanes = edges.shape
    groups = dates // 4
    return pl.pallas_call(
        edge_sums_kernel,
        out_shape=(
            jax.ShapeDtypeStruct((2 * groups, 256, 512), BF16),
            jax.ShapeDtypeStruct((dates, lanes), BF16),
        ),
        scratch_shapes=[
            pltpu.VMEM((256, 512), BF16),
            pltpu.VMEM((groups, 256, 512), BF16),
            pltpu.VMEM((4, slots * ROWS, 256), BF16),
            pltpu.VMEM((4, 4, slots * ROWS, LANES), BF16),
        ],
        compiler_params=pltpu.CompilerParams(vmem_limit_bytes=58 << 20),
        name="edge_sums",
    )(edges, *weights)


def pool_lots(sums, counts, es, ec, lots_owned, w_pool, code, peers, chunk):
    blocks, groups = sums.shape[:2]
    dates = counts.shape[0]
    own = 8
    feats = w_pool.shape[1]
    fixed = (ec, lots_owned, w_pool, code)
    return pl.pallas_call(
        functools.partial(pool_kernel, chunk=chunk),
        grid=(blocks, groups),
        in_specs=[
            pl.BlockSpec((1, 1) + sums.shape[2:], lambda i, g: (i, g, 0, 0, 0)),
            pl.BlockSpec((dates, 256), lambda i, g: (0, i)),
            pl.BlockSpec((2,) + es.shape[1:], lambda i, g: (g, 0, 0)),
        ]
        + [whole(x) for x in fixed],
        out_specs=pl.BlockSpec((LANES // own, own, dates, feats), lambda i, g: (i, 0, 0, 0)),
        out_shape=jax.ShapeDtypeStruct((peers, own, dates, feats), BF16),
        scratch_shapes=[
            pltpu.VMEM((LANES, 256), BF16),
            pltpu.VMEM((dates, LANES, LANES), F32),
            pltpu.VMEM((dates, LANES, 256), BF16),
            pltpu.VMEM((dates, LANES, LANES), BF16),
            pltpu.VMEM((256, 256), BF16),
        ],
        compiler_params=pltpu.CompilerParams(vmem_limit_bytes=56 << 20),
        name=f"pool_{chunk}",
    )(sums, counts, es, *fixed)


def erf_gelu(x):
    return 0.5 * x * (1.0 + lax.erf(x * (1.0 / math.sqrt(2.0))))


def norm_rows(x, gain):
    average = jnp.mean(x, axis=-1, keepdims=True)
    centered = x - average
    variance = jnp.mean(centered * centered, axis=-1, keepdims=True)
    return centered * lax.rsqrt(variance + NORM_EPS) * gain


def attention_kernel(
    e_ref, ln1_ref, wq_ref, wk_ref, wv_ref, wo_ref, ln2_ref, up_ref, down_ref, *rest, last,
):
    if last:
        first_ref, out_ref, enc_ref, q_ref, v_ref, k_ref, mix_ref = rest
    else:
        enc_ref, q_ref, v_ref, k_ref, mix_ref = rest
    peers, own, dates, width = e_ref.shape
    total = peers * dates
    head = width // HEADS
    together = q_ref.shape[0]
    tall = 256
    scale = math.log2(math.e) / math.sqrt(head)

    def rows_of(lot):
        return jnp.concatenate([e_ref[:, lot + l].reshape(total, width) for l in range(together)], axis=0).astype(F32)

    def project(lot):
        normed = norm_rows(rows_of(lot), ln1_ref[...]).astype(BF16)
        weights = jnp.concatenate([wq_ref[...], wv_ref[...]], axis=1)
        both = jnp.dot(normed, weights, preferred_element_type=F32).astype(BF16)
        keys_t = lax.dot_general(wk_ref[...].T, normed, NT, preferred_element_type=F32).astype(BF16)
        for l in range(together):
            here = slice(l * total, (l + 1) * total)
            q_ref[l] = both[here, :width]
            v_ref[l] = both[here, width:]
            k_ref[l] = keys_t[:, here]

    def mix_dates(l):
        lane = lax.broadcasted_iota(jnp.int32, (total, width), 1)
        ones = jnp.ones((total, width), BF16)
        zero = jnp.zeros((total, width), BF16)
        parts = [None] * (total // tall)
        for h in range(HEADS):
            mine = lane // head == h
            queries = jnp.where(mine, q_ref[l], zero)
            values = jnp.concatenate([jnp.where(mine, v_ref[l], zero), ones], axis=1)
            for b in range(total // tall):
                here = slice(b * tall, (b + 1) * tall)
                scores = jnp.dot(queries[here], k_ref[l], preferred_element_type=F32)
                top = jnp.max(scores, axis=1, keepdims=True) * scale
                weights = jnp.exp2(scores * scale - top).astype(BF16)
                mix = jnp.dot(weights, values, preferred_element_type=F32)
                mix = mix[:, :width] * (1.0 / mix[:, width:])
                parts[b] = mix if parts[b] is None else parts[b] + mix
        mix_ref[l] = jnp.concatenate(parts, axis=0).astype(BF16)

    def feed_forward(lot):
        mixture = mix_ref[...].reshape(together * total, width)
        carried = rows_of(lot) + jnp.dot(mixture, wo_ref[...], preferred_element_type=F32)
        normed_two = norm_rows(carried, ln2_ref[...]).astype(BF16)
        hidden = erf_gelu(jnp.dot(normed_two, up_ref[...], preferred_element_type=F32)).astype(BF16)
        encoded = (carried + jnp.dot(hidden, down_ref[...], preferred_element_type=F32)).astype(BF16)
        for l in range(together):
            enc_ref[lot + l] = encoded[l * total : (l + 1) * total].reshape(peers, dates, width)

    @pl.loop(0, own, step=together)
    def _(lot):
        project(lot)

        @pl.loop(0, together, step=2)
        def _(l):
            mix_dates(l)
            mix_dates(l + 1)

        feed_forward(lot)

    if last:
        perm = swap_rows(dates)
        for p in range(0, peers, 2):
            two = jnp.concatenate(
                [
                    jnp.concatenate([first_ref[:, p + s], enc_ref[:, p + s]], axis=0).reshape(2 * own * dates, width)
                    for s in range(2)
                ],
                axis=1,
            )
            y = jnp.dot(perm, two, preferred_element_type=F32).astype(BF16)
            for s in range(2):
                here = slice((p + s) * dates, (p + s + 1) * dates)
                out_ref[here] = y[:, s * width : (s + 1) * width].reshape(dates, 2 * own, width)


def attend(embedded, params, first=None):
    peers, own, dates, width = embedded.shape
    total = peers * dates
    together = 4
    scratch = [
        pltpu.VMEM((together, total, width), BF16),
        pltpu.VMEM((together, total, width), BF16),
        pltpu.VMEM((together, width, total), BF16),
        pltpu.VMEM((together, total, width), BF16),
    ]
    last = first is not None
    mid = (own, peers, dates, width)
    return pl.pallas_call(
        functools.partial(attention_kernel, last=last),
        out_shape=jax.ShapeDtypeStruct((total, 2 * own, width) if last else mid, BF16),
        scratch_shapes=([pltpu.VMEM(mid, BF16)] if last else []) + scratch,
        compiler_params=pltpu.CompilerParams(vmem_limit_bytes=48 << 20),
        name="attend_last" if last else "attend_first",
    )(embedded, *params, *([first] if last else []))


def position_code(day_numbers, model_width):
    lane = lax.broadcasted_iota(jnp.int32, (day_numbers.shape[0], model_width), 1)
    freq_rate = jnp.exp(-(2.0 * (lane // 2).astype(F32) / model_width) * math.log(1000.0))
    phase_angle = day_numbers.astype(F32)[:, None] * freq_rate
    return jnp.where(lane % 2 == 0, jnp.sin(phase_angle), jnp.cos(phase_angle))


def edge_kernel(pix_ref, mask_ref, out_ref):
    bands, slots = pix_ref.shape[:2]
    half = slots // 2
    for p in range(half):
        masks = [jnp.where(mask_ref[p + s * half] > 0, 1.0, 0.0) for s in range(2)]
        out_ref[bands, p] = jnp.concatenate(masks, axis=-1).astype(BF16)
        for b in range(bands):
            two = [pix_ref[b, p + s * half].astype(F32) * masks[s] for s in range(2)]
            out_ref[b, p] = jnp.concatenate(two, axis=-1).astype(BF16)


def edge_rows(edge_pixels, edge_mask):
    bands, slots, dates, blocks = edge_pixels.shape
    return pl.pallas_call(
        edge_kernel,
        out_shape=jax.ShapeDtypeStruct((bands + 1, slots // 2, dates, 2 * blocks), BF16),
        name="edge_rows",
    )(edge_pixels, edge_mask)


def per_device(
    pixels, counts, edge_pixels, edge_mask, straddle_lot, date_days,
    w_first, b_first, w_second, b_second, w_pool, b_pool,
    ln_one, w_query, w_key, w_value, w_out, ln_two, w_up, w_down,
):
    groups = lax.axis_size("group")
    peers = lax.axis_size("date")
    dates = pixels.shape[2]
    width = w_pool.shape[1]
    edges = lax.ppermute(
        edge_rows(edge_pixels, edge_mask), "group", [(i, (i + 1) % groups) for i in range(groups)]
    )
    weights = (w_first, b_first[None], w_second, b_second[None])
    slots = pixels.shape[1]
    blocks = pixels.shape[3] // 256
    own_days = lax.dynamic_slice_in_dim(date_days, lax.axis_index("date") * dates, dates)
    code = position_code(own_days, width) + b_pool
    params = (ln_one[None], w_query, w_key, w_value, w_out, ln_two[None], w_up, w_down)
    sums, turned = own_sums(weights, slots, dates, blocks, pixels=pixels, counts=counts)
    es, ec = edge_sums(edges, weights)
    series = []
    for chunk in range(2):
        if chunk:
            sums = own_sums(weights, slots, dates, blocks, turned=turned)
        pooled = pool_lots(sums, counts, es, ec, straddle_lot[None], w_pool, code, peers, chunk)
        series.append(lax.all_to_all(pooled, "date", split_axis=0, concat_axis=0, tiled=True))
    return attend(series[1], params, attend(series[0], params))


def solution(mesh):
    return jax.shard_map(
        per_device,
        mesh=mesh,
        in_specs=(
            P(None, None, "date", "group"),
            P("date", "group"),
            P(None, None, "date", "group"),
            P(None, "date", "group"),
            P("group"),
        )
        + (P(),) * 15,
        out_specs=P(None, ("group", "date"), None),
        check_vma=False,
    )
```

time: 111 us -> 118 us (1.063)
  Pallas kernels: 80.7 us -> 93.4 us
  waiting for transfers between devices: 3.94 us -> 0.01 us
  other arithmetic: 4.44 us -> 1.49 us
    pallas_call x2 -> x5, Pallas kernels: 40.7 us -> 53.1 us  [the longest x2 28.3 us: own_sums(): pl.pallas_call(first_sums_kernel if first else second_sums_kernel, grid=(...]
    ppermute x1, waiting for transfers between devices: 3.93 us -> 0.01 us  [per_device(): lax.ppermute(edge_rows(edge_pixels, edge_mask), 'group', [(i, (i + 1) % g...]
    unnamed x29 -> x22, local copies, waits for them, and re-layouts: 1.79 us -> 3.5 us
    concatenate x2 -> x0, other arithmetic: 1.55 us -> none  [the longest x1 0.84 us: per_device(): jnp.concatenate([straddle_lot] * 3 + [jnp.full_like(straddle_lot, -1)])]
    another operation x4 -> x0, other arithmetic: 1.34 us -> none  [the longest x2 0.67 us: pixel_weights(): bias = jnp.tile(jnp.stack(three_parts(b_second)), (1, 4))]
  transfers between devices with their start and end apart: 3 -> 3, of which waited for: 1 -> 0; matrix products, arithmetic and copies ran while one was open for 5% -> 4% of each run, Pallas kernels for 35% -> 49%
where the time goes in v3:
time: 118 us; the launch traced here: 116 us
  Pallas kernels  93.4 us (79%)
  starting transfers between devices  17.9 us (15%)
  local copies, waits for them, and re-layouts  3.5 us (3%)
  other arithmetic  1.49 us (1%)
    pallas_call x2, Pallas kernels, attend(): pl.pallas_call(functools.partial(attention_kernel, last=last), out_shape=...  38.4 us
    pallas_call x2, Pallas kernels, own_sums(): pl.pallas_call(first_sums_kernel if first else second_sums_kernel, grid=(...  28.3 us
    pallas_call x2, Pallas kernels, pool_lots(): pl.pallas_call(functools.partial(pool_kernel, chunk=chunk), grid=(blocks,...  20.5 us
    all_to_all x2, starting transfers between devices, per_device(): lax.all_to_all(pooled, 'date', split_axis=0, concat_axis=0, tiled=True)  15.4 us
    pallas_call x1, Pallas kernels, edge_sums(): pl.pallas_call(edge_sums_kernel, out_shape=(jax.ShapeDtypeStruct((2 * gro...  4.38 us
    unnamed x22, local copies, waits for them, and re-layouts  3.5 us
    ppermute x1, starting transfers between devices, per_device(): lax.ppermute(edge_rows(edge_pixels, edge_mask), 'group', [(i, (i + 1) % g...  2.47 us
  transfers between devices with their start and end apart: 3, of which 0 were waited for; matrix products, arithmetic and copies ran while one was open for 4% of the time, Pallas kernels for 49%

profile of v3, /device:TPU:1, one launch (start us, length us, event | category | flops | bytes accessed | tf_op | source)
XLA Modules:
  0.0 116.5 jit_solution(8875883969517879078)
XLA Ops:
  0.0 1.8 %edge_rows.1 = bf16[14,4,16,128]{3,2,1,0:T(8,128)(2,1)} custom-call(bf16[13,8,16,64]{3,2,1,0:T(8,128)(2,1)} %pix_ref.3, s32[8,16,64]{2,1,0:T(8,128)} %mask_ref.1), custom_call_target="tpu_custom_call" | custom-call | tf_op jit(solution)/shard_map/edge_rows/pallas_call | solution.py:480
  1.8 2.5 %collective-permute-start = (bf16[14,4,16,128]{3,2,1,0:T(8,128)(2,1)}, bf16[14,4,16,128]{3,2,1,0:T(8,128)(2,1)S(1)}, u32[]{:S(2)}, u32[]{:S(2)}) collective-permute-start(bf16[14,4,16,128]{3,2,1,0:T(8,128)(2,1)} %edge_rows.1), channel_id=1, source_target_pairs={{0,32},{32,64},{64,96},{96,128},{128,160},{160,192},{192,224},{224... | collective-permute-start | bytes 688136 | tf_op jit(solution)/shard_map/ppermute | solution.py:496
  4.3 0.8 dynamic-slice_convert_fusion
  5.1 1.4 %copy.22.ws_ref = bf16[128,32]{1,0:T(8,128)(2,1)} copy(bf16[128,32]{0,1:T(8,128)(2,1)} %param.28) | data formatting | bytes 16384 | tf_op args[8]
  6.5 1.4 %copy.21.wf_ref = bf16[32,13]{1,0:T(8,128)(2,1)} copy(bf16[32,13]{0,1:T(8,128)(2,1)} %param.26) | data formatting | bytes 1664 | tf_op args[6]
  7.9 15.3 %first_sums.1 = (f32[2,4,2,128,512]{4,3,2,1,0:T(8,128)}, bf16[2,4,768,256]{3,2,1,0:T(8,128)(2,1)}) custom-call(bf16[13,24,16,512]{3,2,1,0:T(8,128)(2,1)} %pix_ref.2, s32[16,512]{1,0:T(8,128)} %cnt_ref.5, bf16[32,13]{1,0:T(8,128)(2,1)} %copy.21.wf_ref, f32[1,32]{1,0:T(1,128)} %bitcast.9, bf16[128,32]{1,0:T(8,128)(2,1)} %copy.22.ws_ref, f32[1,128]{1,0:T(1,128)} %bitcast.12), custom_call_target="tpu_custom_call" | custom-call | tf_op jit(solution)/shard_map/first_sums/pallas_call | solution.py:284
  23.2 0.7 select_add_fusion.code_ref
  23.9 0.0 collective-permute-done.edge_ref
  23.9 0.7 copy-done.8
  24.6 4.4 %edge_sums.1 = (bf16[8,256,512]{2,1,0:T(8,128)(2,1)}, bf16[16,128]{1,0:T(8,128)(2,1)}) custom-call(bf16[14,4,16,128]{3,2,1,0:T(8,128)(2,1)} %copy-done.8, bf16[32,13]{1,0:T(8,128)(2,1)} %copy.21.wf_ref, f32[1,32]{1,0:T(1,128)} %bitcast.10, bf16[128,32]{1,0:T(8,128)(2,1)} %copy.22.ws_ref, f32[1,128]{1,0:T(1,128)} %bitcast.13), custom_call_target="tpu_custom_call" | custom-call | tf_op jit(solution)/shard_map/edge_sums/pallas_call | solution.py:299
  29.0 10.2 %pool_0.1 = bf16[32,8,16,128]{3,2,1,0:T(8,128)(2,1)} custom-call(f32[2,4,2,128,512]{4,3,2,1,0:T(8,128)} %get-tuple-element.12.sums_ref, s32[16,512]{1,0:T(8,128)} %cnt_ref.5, bf16[8,256,512]{2,1,0:T(8,128)(2,1)} %get-tuple-element.10.es_ref, bf16[16,128]{1,0:T(8,128)(2,1)} %get-tuple-element.11.ec_ref, s32[1,64]{1,0:T(1,128)} %bitcast.15, ...), custom_call_target="tpu_custom_call" | custom-call | tf_op jit(solution)/shard_map/pool_0/pallas_call | solution.py:322
  39.2 8.0 %all-to-all-start.1 = ((bf16[32,8,16,128]{3,2,1,0:T(8,128)(2,1)}), bf16[32,8,16,128]{3,2,1,0:T(8,128)(2,1)S(1)}, u32[]{:S(2)}, u32[]{:S(2)}) async-start(bf16[32,8,16,128]{3,2,1,0:T(8,128)(2,1)} %pool_0.1), calls=%async_computation.1 | async-start | bytes 2097152 | tf_op jit(solution)/shard_map/all_to_all | solution.py:512
  47.2 13.0 %second_sums.1.sums_ref = f32[2,4,2,128,512]{4,3,2,1,0:T(8,128)} custom-call(bf16[2,4,768,256]{3,2,1,0:T(8,128)(2,1)} %get-tuple-element.9.xt_ref, bf16[32,13]{1,0:T(8,128)(2,1)} %copy.21.wf_ref, f32[1,32]{1,0:T(1,128)} %bitcast.11, bf16[128,32]{1,0:T(8,128)(2,1)} %copy.22.ws_ref, f32[1,128]{1,0:T(1,128)} %bitcast.14), custom_call_target="tpu_custom_call" | custom-call | tf_op jit(solution)/shard_map/second_sums/pallas_call | solution.py:284
  60.2 0.0 copy-start.3
  60.2 0.0 copy-start.4
  60.2 0.0 copy-start.5
  60.2 0.0 copy-start.6
  60.2 0.0 copy-start.7
  60.2 10.3 %pool_1.1 = bf16[32,8,16,128]{3,2,1,0:T(8,128)(2,1)} custom-call(f32[2,4,2,128,512]{4,3,2,1,0:T(8,128)} %second_sums.1.sums_ref, s32[16,512]{1,0:T(8,128)} %cnt_ref.5, bf16[8,256,512]{2,1,0:T(8,128)(2,1)} %get-tuple-element.10.es_ref, bf16[16,128]{1,0:T(8,128)(2,1)} %get-tuple-element.11.ec_ref, s32[1,64]{1,0:T(1,128)} %bitcast.16, bf16[256,128]{1,0:T(8,128)(2,1)} %wp_ref.3, ...), custom_call_target="tpu_custom_call" | custom-call | tf_op jit(solution)/shard_map/pool_1/pallas_call | solution.py:322
  70.5 0.0 all-to-all-done.1.e_ref
  70.5 7.4 %all-to-all-start = ((bf16[32,8,16,128]{3,2,1,0:T(8,128)(2,1)}), bf16[32,8,16,128]{3,2,1,0:T(8,128)(2,1)S(1)}, u32[]{:S(2)}, u32[]{:S(2)}) async-start(bf16[32,8,16,128]{3,2,1,0:T(8,128)(2,1)} %pool_1.1), calls=%async_computation | async-start | bytes 2097152 | tf_op jit(solution)/shard_map/all_to_all | solution.py:512
  78.0 18.2 %attend_first.1.rest_0_ = bf16[8,32,16,128]{3,2,1,0:T(8,128)(2,1)S(1)} custom-call(bf16[32,8,16,128]{3,2,1,0:T(8,128)(2,1)S(1)} %all-to-all-done.1.e_ref, f32[1,128]{1,0:T(1,128)S(1)} %bitcast.5, bf16[128,128]{1,0:T(8,128)(2,1)S(1)} %copy-done.2, bf16[128,128]{1,0:T(8,128)(2,1)S(1)} %copy-done.3, bf16[128,128]{1,0:T(8,128)(2,1)S(1)} %copy-done.4, ...), custom_call_target="tpu_custom_call" | custom-call | tf_op jit(solution)/shard_map/attend_first/pallas_call | solution.py:451
  96.2 0.0 all-to-all-done.e_ref
  96.2 20.2 %attend_last.1 = bf16[512,16,128]{2,1,0:T(8,128)(2,1)} custom-call(bf16[32,8,16,128]{3,2,1,0:T(8,128)(2,1)S(1)} %all-to-all-done.e_ref, f32[1,128]{1,0:T(1,128)S(1)} %bitcast.6, bf16[128,128]{1,0:T(8,128)(2,1)S(1)} %copy-done.2, bf16[128,128]{1,0:T(8,128)(2,1)S(1)} %copy-done.3, bf16[128,128]{1,0:T(8,128)(2,1)S(1)} %copy-done.4, ...), custom_call_target="tpu_custom_call" | custom-call | tf_op jit(solution)/shard_map/attend_last/pallas_call | solution.py:451
  (17 shorter events, 0.0 us)
Async XLA Ops:
  0.0 23.2 %copy-start.9 = (f32[128]{0:T(128)S(1)}, f32[128]{0:T(128)}, u32[]{:S(2)}) copy-start(f32[128]{0:T(128)} %param.31) | copy-start | bytes 1540
  1.8 22.1 %collective-permute-start = (bf16[14,4,16,128]{3,2,1,0:T(8,128)(2,1)}, bf16[14,4,16,128]{3,2,1,0:T(8,128)(2,1)S(1)}, u32[]{:S(2)}, u32[]{:S(2)}) collective-permute-start(bf16[14,4,16,128]{3,2,1,0:T(8,128)(2,1)} %edge_rows.1), channel_id=1, source_target_pairs={{0,32},{32,64},{64,96},{96,128},{128,160},{160,192},{192,224},{224... | collective-permute-start | bytes 688136 | tf_op jit(solution)/shard_map/ppermute | solution.py:496
  23.9 0.7 copy-start.8
  39.2 31.4 %all-to-all-start.1 = ((bf16[32,8,16,128]{3,2,1,0:T(8,128)(2,1)}), bf16[32,8,16,128]{3,2,1,0:T(8,128)(2,1)S(1)}, u32[]{:S(2)}, u32[]{:S(2)}) async-start(bf16[32,8,16,128]{3,2,1,0:T(8,128)(2,1)} %pool_0.1), calls=%async_computation.1 | async-start | bytes 2097152 | tf_op jit(solution)/shard_map/all_to_all | solution.py:512
  60.2 17.8 %copy-start = (bf16[128,512]{1,0:T(8,128)(2,1)S(1)}, bf16[128,512]{1,0:T(8,128)(2,1)}, u32[]{:S(2)}) copy-start(bf16[128,512]{1,0:T(8,128)(2,1)} %up_ref.3) | copy-start | bytes 393220
  60.2 17.8 %copy-start.1 = (bf16[512,128]{1,0:T(8,128)(2,1)S(1)}, bf16[512,128]{1,0:T(8,128)(2,1)}, u32[]{:S(2)}) copy-start(bf16[512,128]{1,0:T(8,128)(2,1)} %down_ref.3) | copy-start | bytes 393220
  60.2 17.8 %copy-start.2 = (bf16[128,128]{1,0:T(8,128)(2,1)S(1)}, bf16[128,128]{1,0:T(8,128)(2,1)}, u32[]{:S(2)}) copy-start(bf16[128,128]{1,0:T(8,128)(2,1)} %wq_ref.3) | copy-start | bytes 98308
  60.2 17.8 %copy-start.3 = (bf16[128,128]{1,0:T(8,128)(2,1)S(1)}, bf16[128,128]{1,0:T(8,128)(2,1)}, u32[]{:S(2)}) copy-start(bf16[128,128]{1,0:T(8,128)(2,1)} %wk_ref.3) | copy-start | bytes 98308
  60.2 17.8 %copy-start.4 = (bf16[128,128]{1,0:T(8,128)(2,1)S(1)}, bf16[128,128]{1,0:T(8,128)(2,1)}, u32[]{:S(2)}) copy-start(bf16[128,128]{1,0:T(8,128)(2,1)} %wv_ref.3) | copy-start | bytes 98308
  60.2 17.8 %copy-start.5 = (bf16[128,128]{1,0:T(8,128)(2,1)S(1)}, bf16[128,128]{1,0:T(8,128)(2,1)}, u32[]{:S(2)}) copy-start(bf16[128,128]{1,0:T(8,128)(2,1)} %wo_ref.3) | copy-start | bytes 98308
  60.2 17.8 %copy-start.6 = (f32[128]{0:T(128)S(1)}, f32[128]{0:T(128)}, u32[]{:S(2)}) copy-start(f32[128]{0:T(128)} %param.32) | copy-start | bytes 1540
  60.2 17.8 %copy-start.7 = (f32[128]{0:T(128)S(1)}, f32[128]{0:T(128)}, u32[]{:S(2)}) copy-start(f32[128]{0:T(128)} %param.37) | copy-start | bytes 1540
  70.5 25.7 %all-to-all-start = ((bf16[32,8,16,128]{3,2,1,0:T(8,128)(2,1)}), bf16[32,8,16,128]{3,2,1,0:T(8,128)(2,1)S(1)}, u32[]{:S(2)}, u32[]{:S(2)}) async-start(bf16[32,8,16,128]{3,2,1,0:T(8,128)(2,1)} %pool_1.1), calls=%async_computation | async-start | bytes 2097152 | tf_op jit(solution)/shard_map/all_to_all | solution.py:512

commit v4 on v3

v4 whole, which is shorter than its diff:
```python
import functools
import math

import jax
import jax.numpy as jnp
from jax import lax
from jax.experimental import pallas as pl
from jax.experimental.pallas import tpu as pltpu
from jax.sharding import PartitionSpec as P

HEADS = 4
VAR_FLOOR = 0.05
NORM_EPS = 1e-05
F32 = jnp.float32
BF16 = jnp.bfloat16
LANES = 128


def relu_bf16(values):
    return jnp.maximum(values, 0.0).astype(BF16)


NT = (((1,), (1,)), ((), ()))


def ones_where(condition):
    return jnp.where(condition, 1.0, 0.0).astype(BF16)


def grid_of(shape):
    return lax.broadcasted_iota(jnp.int32, shape, 0), lax.broadcasted_iota(jnp.int32, shape, 1)


def three_parts(values):
    parts = []
    for _ in range(3):
        parts.append(values.astype(BF16))
        values = values - parts[-1].astype(F32)
    return parts


def spread_weights(wf_ref, bf_ref, ws_ref, bs_ref, w1_ref, w2_ref):
    bands, h1 = wf_ref.shape
    feats = ws_ref.shape[1]
    groups = w2_ref.shape[0]
    dates = 4 * groups
    wide = dates * h1
    row, col = grid_of((h1, wide))
    repeat = ones_where(row == col % h1)
    taps = jnp.dot(wf_ref[...], repeat, preferred_element_type=F32)
    row, col = grid_of((dates, wide))
    keep = row == col // h1
    for b in range(bands):
        line = jnp.broadcast_to(taps[b : b + 1], (dates, wide))
        w1_ref[b * dates : (b + 1) * dates, :] = jnp.where(keep, line, 0.0).astype(BF16)
    for part, values in enumerate(three_parts(jnp.broadcast_to(bf_ref[...], (dates, h1)))):
        line = jnp.dot(values, repeat, preferred_element_type=F32)
        start = (bands + part) * dates
        w1_ref[start : start + dates, :] = jnp.where(keep, line, 0.0).astype(BF16)
    stacked = jnp.concatenate([ws_ref[...].astype(F32)] * 4, axis=0)
    row_two, col_two = grid_of((4 * h1, 4 * feats))
    body = jnp.where(row_two // h1 == col_two // feats, jnp.concatenate([stacked] * 4, axis=1), 0.0).astype(BF16)
    lines = [part.astype(F32) for part in three_parts(jnp.broadcast_to(bs_ref[...], (dates, feats)))]
    lines = [jnp.concatenate([line] * 4, axis=1) for line in lines]
    row, col = grid_of((dates, 4 * feats))
    gap = 256 - 3 * dates
    for g in range(groups):
        w2_ref[g, : 4 * h1, :] = body
        w2_ref[g, 4 * h1 : gap, :] = jnp.zeros((gap - 4 * h1, 4 * feats), BF16)
        for part in range(3):
            start = gap + part * dates
            w2_ref[g, start : start + dates, :] = jnp.where(row == 4 * g + col // feats, lines[part], 0.0).astype(BF16)


def swap_rows(size):
    row = lax.broadcasted_iota(jnp.int32, (size * size, size * size), 0)
    col = lax.broadcasted_iota(jnp.int32, (size * size, size * size), 1)
    return jnp.where(col == (row % size) * size + row // size, 1.0, 0.0).astype(BF16)


ROWS = 32


def first_layer(xt, h_ref, w1_ref, count):
    def finish(r, z):
        z = relu_bf16(z)
        for g in range(4):
            h_ref[g, r, : count * ROWS, :] = z[:, g * LANES : (g + 1) * LANES]

    before = None
    for r in range(4):
        z = jnp.dot(xt(r), w1_ref[...], preferred_element_type=F32)
        if before is not None:
            finish(r - 1, before)
        before = z
    finish(3, before)


def second_layer(xt, h_ref, w2_ref, g, r, count):
    a = jnp.concatenate([h_ref[g, r, : count * ROWS, :], xt(r)[:, LANES:]], axis=1)
    return jnp.dot(a, w2_ref[g], preferred_element_type=F32)


def add_slots(z, count, lanes):
    total = square = None
    for p in range(count):
        part = jnp.maximum(z[p * ROWS : (p + 1) * ROWS, lanes], 0.0)
        total = part if total is None else total + part
        square = part * part if square is None else square + part * part
    return total, square


def halves(values):
    return [
        jnp.concatenate([values[k + 8 * c : k + 8 * c + 8] for k in range(0, LANES, 16)], axis=0) for c in range(2)
    ]


def lay_out_kernel(pix_ref, cnt_ref, first_ref, second_ref):
    bands, slots = pix_ref.shape[:2]
    counts = cnt_ref[...]
    for p in range(slots):
        mask = ones_where(counts > p)
        for side in range(2):
            lanes = slice(side * LANES, (side + 1) * LANES)
            m = mask[:, lanes]
            x = jnp.concatenate([pix_ref[b, p, :, lanes] * m for b in range(bands)] + [m] * 3, axis=0)
            for ref, xt in zip((first_ref, second_ref), halves(x.astype(F32).T)):
                xt = xt.astype(BF16)
                for r in range(2):
                    ref[0, 2 * side + r, p * ROWS : (p + 1) * ROWS, :] = xt[r * ROWS : (r + 1) * ROWS]


def pixel_kernel(
    xt_ref, cnt_ref, edge_ref, lot_ref, wf_ref, bf_ref, ws_ref, bs_ref, wp_ref, code_ref, out_ref,
    w1_ref, w2_ref, ext_ref, h_ref, es_ref, ec_ref, chosen_ref, init_ref, inv_ref, pool_ref, e_ref, perm_ref, *, chunk,
):
    block = pl.program_id(0)
    dates, lots = cnt_ref.shape
    slots = xt_ref.shape[2] // ROWS
    groups = w2_ref.shape[0]
    mine = lambda r: xt_ref[0, r]
    lot = jnp.concatenate([lot_ref[...], lot_ref[...]], axis=1)

    @pl.when(block == 0)
    def _():
        spread_weights(wf_ref, bf_ref, ws_ref, bs_ref, w1_ref, w2_ref)
        perm_ref[...] = swap_rows(dates)
        bands = edge_ref.shape[0] - 1
        edge_slots = edge_ref.shape[1]
        half = LANES // 2
        theirs = lambda r: ext_ref[r]
        ec = jnp.zeros((dates, LANES), F32)
        for p in range(edge_slots):
            mask = edge_ref[bands, p]
            xt = jnp.concatenate([edge_ref[b, p] for b in range(bands)] + [mask] * 3, axis=0).T
            for r in range(4):
                ext_ref[r, p * ROWS : (p + 1) * ROWS, :] = xt[r * ROWS : (r + 1) * ROWS]
            ec = ec + mask.astype(F32)
        ec_ref[...] = ec.astype(BF16)
        first_layer(theirs, h_ref, w1_ref, edge_slots)
        es_ref[:, 3 * half :, :] = jnp.zeros((es_ref.shape[0], half, es_ref.shape[2]), BF16)

        def settle(g, zs):
            for c in range(2):
                lanes = slice(256 * c, 256 * (c + 1))
                stats = [add_slots(zs[r], edge_slots, lanes) for r in range(4)]
                for k in range(2):
                    for r in range(2):
                        v = stats[r][k] + stats[r + 2][k]
                        for part, cut in enumerate(three_parts(v)):
                            here = slice(part * half + r * ROWS, part * half + (r + 1) * ROWS)
                            es_ref[2 * g + c, here, 256 * k : 256 * (k + 1)] = cut

        before = None
        for g in range(groups):
            zs = [second_layer(theirs, h_ref, w2_ref, g, r, edge_slots) for r in range(4)]
            if before is not None:
                settle(g - 1, before)
            before = zs
        settle(groups - 1, before)

    lane = lax.broadcasted_iota(jnp.int32, lot.shape, 1)
    four = jnp.concatenate([lot, jnp.where(lane < LANES // 2, lot, -1)], axis=1)
    row = lax.broadcasted_iota(jnp.int32, (LANES, 256), 0)
    chosen_ref[...] = ones_where(block * lots + (row // 8) * 16 + 8 * chunk + row % 8 == four)
    lot_rows = lax.broadcasted_iota(jnp.int32, (lots, LANES), 0) + block * lots
    extra = lax.dot_general(ec_ref[...], ones_where(lot_rows == lot), NT, preferred_element_type=F32)
    inverse = 1.0 / (cnt_ref[...].astype(F32) + extra)
    inv_t = jnp.concatenate([halves(inverse[:, s * LANES : (s + 1) * LANES].T)[chunk] for s in range(2)], axis=0)
    for d in range(dates):
        inv_ref[d] = jnp.broadcast_to(inv_t[:, d : d + 1], (LANES, LANES))
    first_layer(mine, h_ref, w1_ref, slots)

    def finish(g, r, z):
        here = slice(r * ROWS, (r + 1) * ROWS)
        for c in range(2):
            total, square = add_slots(z, slots, slice(256 * c, 256 * (c + 1)))
            total = total + init_ref[c, here, :256]
            square = square + init_ref[c, here, 256:]
            for k in range(2):
                d = 4 * g + 2 * c + k
                inv = inv_ref[d, here, :]
                lanes = slice(k * LANES, (k + 1) * LANES)
                average = total[:, lanes] * inv
                spread = jnp.maximum(square[:, lanes] * inv - average * average, VAR_FLOOR)
                spread = spread * lax.rsqrt(spread)
                pool_ref[d, here, :LANES] = average.astype(BF16)
                pool_ref[d, here, LANES:] = spread.astype(BF16)

    def embed(g):
        four = pool_ref[4 * g : 4 * g + 4].reshape(4 * LANES, 256)
        e = jnp.dot(four, wp_ref[...], preferred_element_type=F32)
        for k in range(4):
            d = 4 * g + k
            e_ref[d] = (e[k * LANES : (k + 1) * LANES] + code_ref[d : d + 1, :]).astype(BF16)

    before = None
    for g in range(groups):
        for r in range(4):
            z = second_layer(mine, h_ref, w2_ref, g, r, slots)
            if before is not None:
                finish(*before)
            if r == 0:
                for c in range(2):
                    init_ref[c] = jnp.dot(chosen_ref[...], es_ref[2 * g + c], preferred_element_type=F32)
            if r == 1 and g > 0:
                embed(g - 1)
            before = (g, r, z)
    finish(*before)
    embed(groups - 1)

    for k in range(0, LANES, 32):
        both = jnp.concatenate(
            [e_ref[:, k + s : k + s + 16, :].reshape(dates * 16, LANES) for s in (0, 16)], axis=1
        )
        y = jnp.dot(perm_ref[...], both, preferred_element_type=F32).astype(BF16)
        for s in range(2):
            here = slice(k // 8 + 2 * s, k // 8 + 2 * s + 2)
            out_ref[here] = y[:, s * LANES : (s + 1) * LANES].reshape(2, 8, dates, LANES)


def whole(x):
    return pl.BlockSpec(x.shape, lambda *_: (0,) * x.ndim, pipeline_mode=pl.Buffered(1))


def lay_out(pixels, counts):
    bands, slots, dates, lots = pixels.shape
    blocks = lots // 256
    laid = jax.ShapeDtypeStruct((blocks, 4, slots * ROWS, 256), BF16)
    laid_spec = pl.BlockSpec((1,) + laid.shape[1:], lambda i: (i, 0, 0, 0))
    return pl.pallas_call(
        lay_out_kernel,
        grid=(blocks,),
        in_specs=[
            pl.BlockSpec((bands, slots, dates, 256), lambda i: (0, 0, 0, i)),
            pl.BlockSpec((dates, 256), lambda i: (0, i)),
        ],
        out_specs=(laid_spec, laid_spec),
        out_shape=(laid, laid),
        compiler_params=pltpu.CompilerParams(vmem_limit_bytes=58 << 20),
        name="lay_out",
    )(pixels, counts)


def pool_lots(laid, counts, edges, lots_owned, weights, w_pool, code, peers, chunk):
    blocks, _, tall, _ = laid.shape
    edge_slots = edges.shape[1]
    dates = counts.shape[0]
    groups = dates // 4
    own = 8
    feats = w_pool.shape[1]
    fixed = (edges, lots_owned, *weights, w_pool, code)
    return pl.pallas_call(
        functools.partial(pixel_kernel, chunk=chunk),
        grid=(blocks,),
        in_specs=[
            pl.BlockSpec((1,) + laid.shape[1:], lambda i: (i, 0, 0, 0)),
            pl.BlockSpec((dates, 256), lambda i: (0, i)),
        ]
        + [whole(x) for x in fixed],
        out_specs=pl.BlockSpec((LANES // own, own, dates, feats), lambda i: (i, 0, 0, 0)),
        out_shape=jax.ShapeDtypeStruct((peers, own, dates, feats), BF16),
        scratch_shapes=[
            pltpu.VMEM((256, 512), BF16),
            pltpu.VMEM((groups, 256, 512), BF16),
            pltpu.VMEM((4, edge_slots * ROWS, 256), BF16),
            pltpu.VMEM((4, 4, tall, LANES), BF16),
            pltpu.VMEM((2 * groups, 256, 512), BF16),
            pltpu.VMEM((dates, LANES), BF16),
            pltpu.VMEM((LANES, 256), BF16),
            pltpu.VMEM((2, LANES, 512), F32),
            pltpu.VMEM((dates, LANES, LANES), F32),
            pltpu.VMEM((dates, LANES, 256), BF16),
            pltpu.VMEM((dates, LANES, LANES), BF16),
            pltpu.VMEM((256, 256), BF16),
        ],
        compiler_params=pltpu.CompilerParams(vmem_limit_bytes=58 << 20),
        name=f"pixel_pool_{chunk}",
    )(laid, counts, *fixed)


def erf_gelu(x):
    return 0.5 * x * (1.0 + lax.erf(x * (1.0 / math.sqrt(2.0))))


def norm_rows(x, gain):
    average = jnp.mean(x, axis=-1, keepdims=True)
    centered = x - average
    variance = jnp.mean(centered * centered, axis=-1, keepdims=True)
    return centered * lax.rsqrt(variance + NORM_EPS) * gain


def attention_kernel(
    e_ref, ln1_ref, wq_ref, wk_ref, wv_ref, wo_ref, ln2_ref, up_ref, down_ref, *rest, last,
):
    if last:
        first_ref, out_ref, enc_ref, q_ref, v_ref, k_ref, mix_ref = rest
    else:
        enc_ref, q_ref, v_ref, k_ref, mix_ref = rest
    peers, own, dates, width = e_ref.shape
    total = peers * dates
    head = width // HEADS
    together = q_ref.shape[0]
    tall = 256
    scale = math.log2(math.e) / math.sqrt(head)

    def rows_of(lot):
        return jnp.concatenate([e_ref[:, lot + l].reshape(total, width) for l in range(together)], axis=0).astype(F32)

    def project(lot):
        normed = norm_rows(rows_of(lot), ln1_ref[...]).astype(BF16)
        weights = jnp.concatenate([wq_ref[...], wv_ref[...]], axis=1)
        both = jnp.dot(normed, weights, preferred_element_type=F32).astype(BF16)
        keys_t = lax.dot_general(wk_ref[...].T, normed, NT, preferred_element_type=F32).astype(BF16)
        for l in range(together):
            here = slice(l * total, (l + 1) * total)
            q_ref[l] = both[here, :width]
            v_ref[l] = both[here, width:]
            k_ref[l] = keys_t[:, here]

    def mix_dates(l):
        lane = lax.broadcasted_iota(jnp.int32, (total, width), 1)
        ones = jnp.ones((total, width), BF16)
        zero = jnp.zeros((total, width), BF16)
        parts = [None] * (total // tall)
        for h in range(HEADS):
            mine = lane // head == h
            queries = jnp.where(mine, q_ref[l], zero)
            values = jnp.concatenate([jnp.where(mine, v_ref[l], zero), ones], axis=1)
            for b in range(total // tall):
                here = slice(b * tall, (b + 1) * tall)
                scores = jnp.dot(queries[here], k_ref[l], preferred_element_type=F32)
                top = jnp.max(scores, axis=1, keepdims=True) * scale
                weights = jnp.exp2(scores * scale - top).astype(BF16)
                mix = jnp.dot(weights, values, preferred_element_type=F32)
                mix = mix[:, :width] * (1.0 / mix[:, width:])
                parts[b] = mix if parts[b] is None else parts[b] + mix
        mix_ref[l] = jnp.concatenate(parts, axis=0).astype(BF16)

    def feed_forward(lot):
        mixture = mix_ref[...].reshape(together * total, width)
        carried = rows_of(lot) + jnp.dot(mixture, wo_ref[...], preferred_element_type=F32)
        normed_two = norm_rows(carried, ln2_ref[...]).astype(BF16)
        hidden = erf_gelu(jnp.dot(normed_two, up_ref[...], preferred_element_type=F32)).astype(BF16)
        encoded = (carried + jnp.dot(hidden, down_ref[...], preferred_element_type=F32)).astype(BF16)
        for l in range(together):
            enc_ref[lot + l] = encoded[l * total : (l + 1) * total].reshape(peers, dates, width)

    @pl.loop(0, own, step=together)
    def _(lot):
        project(lot)

        for l in range(together):
            mix_dates(l)

        feed_forward(lot)

    if last:
        perm = swap_rows(dates)
        for p in range(0, peers, 2):
            two = jnp.concatenate(
                [
                    jnp.concatenate([first_ref[:, p + s], enc_ref[:, p + s]], axis=0).reshape(2 * own * dates, width)
                    for s in range(2)
                ],
                axis=1,
            )
            y = jnp.dot(perm, two, preferred_element_type=F32).astype(BF16)
            for s in range(2):
                here = slice((p + s) * dates, (p + s + 1) * dates)
                out_ref[here] = y[:, s * width : (s + 1) * width].reshape(dates, 2 * own, width)


def attend(embedded, params, first=None):
    peers, own, dates, width = embedded.shape
    total = peers * dates
    together = 4
    scratch = [
        pltpu.VMEM((together, total, width), BF16),
        pltpu.VMEM((together, total, width), BF16),
        pltpu.VMEM((together, width, total), BF16),
        pltpu.VMEM((together, total, width), BF16),
    ]
    last = first is not None
    mid = (own, peers, dates, width)
    return pl.pallas_call(
        functools.partial(attention_kernel, last=last),
        out_shape=jax.ShapeDtypeStruct((total, 2 * own, width) if last else mid, BF16),
        scratch_shapes=([pltpu.VMEM(mid, BF16)] if last else []) + scratch,
        compiler_params=pltpu.CompilerParams(vmem_limit_bytes=48 << 20),
        name="attend_last" if last else "attend_first",
    )(embedded, *params, *([first] if last else []))


def position_code(day_numbers, model_width):
    lane = lax.broadcasted_iota(jnp.int32, (day_numbers.shape[0], model_width), 1)
    freq_rate = jnp.exp(-(2.0 * (lane // 2).astype(F32) / model_width) * math.log(1000.0))
    phase_angle = day_numbers.astype(F32)[:, None] * freq_rate
    return jnp.where(lane % 2 == 0, jnp.sin(phase_angle), jnp.cos(phase_angle))


def edge_kernel(pix_ref, mask_ref, out_ref):
    bands, slots = pix_ref.shape[:2]
    half = slots // 2
    for p in range(half):
        masks = [jnp.where(mask_ref[p + s * half] > 0, 1.0, 0.0) for s in range(2)]
        out_ref[bands, p] = jnp.concatenate(masks, axis=-1).astype(BF16)
        for b in range(bands):
            two = [pix_ref[b, p + s * half].astype(F32) * masks[s] for s in range(2)]
            out_ref[b, p] = jnp.concatenate(two, axis=-1).astype(BF16)


def edge_rows(edge_pixels, edge_mask):
    bands, slots, dates, blocks = edge_pixels.shape
    return pl.pallas_call(
        edge_kernel,
        out_shape=jax.ShapeDtypeStruct((bands + 1, slots // 2, dates, 2 * blocks), BF16),
        name="edge_rows",
    )(edge_pixels, edge_mask)


def per_device(
    pixels, counts, edge_pixels, edge_mask, straddle_lot, date_days,
    w_first, b_first, w_second, b_second, w_pool, b_pool,
    ln_one, w_query, w_key, w_value, w_out, ln_two, w_up, w_down,
):
    groups = lax.axis_size("group")
    peers = lax.axis_size("date")
    dates = pixels.shape[2]
    width = w_pool.shape[1]
    edges = lax.ppermute(
        edge_rows(edge_pixels, edge_mask), "group", [(i, (i + 1) % groups) for i in range(groups)]
    )
    weights = (w_first.T, b_first[None], w_second.T, b_second[None])
    own_days = lax.dynamic_slice_in_dim(date_days, lax.axis_index("date") * dates, dates)
    code = position_code(own_days, width) + b_pool
    params = (ln_one[None], w_query, w_key, w_value, w_out, ln_two[None], w_up, w_down)
    series = []
    for chunk, laid in enumerate(lay_out(pixels, counts)):
        pooled = pool_lots(laid, counts, edges, straddle_lot[None], weights, w_pool, code, peers, chunk)
        series.append(lax.all_to_all(pooled, "date", split_axis=0, concat_axis=0, tiled=True))
    return attend(series[1], params, attend(series[0], params))


def solution(mesh):
    return jax.shard_map(
        per_device,
        mesh=mesh,
        in_specs=(
            P(None, None, "date", "group"),
            P("date", "group"),
            P(None, None, "date", "group"),
            P(None, "date", "group"),
            P("group"),
        )
        + (P(),) * 15,
        out_specs=P(None, ("group", "date"), None),
        check_vma=False,
    )
```

time: 118 us -> 95.2 us (0.81); the launches traced: 116 us -> 94.9 us
  Pallas kernels: 93.4 us -> 71.2 us
  waiting for transfers between devices: 0.01 us -> 5.25 us
  local copies, waits for them, and re-layouts: 3.5 us -> 0.73 us
  starting transfers between devices: 17.9 us -> 16.1 us
    pallas_call x5 -> x3, Pallas kernels: 53.1 us -> 34.7 us  [the longest x2 29.4 us: pool_lots(): pl.pallas_call(functools.partial(pixel_kernel, chunk=chunk), grid=(blocks...]
    pallas_call x2, Pallas kernels: 38.4 us -> 34.6 us  [attend(): pl.pallas_call(functools.partial(attention_kernel, last=last), out_shape=...]
    unnamed x22 -> x20, local copies, waits for them, and re-layouts: 3.5 us -> 0.73 us
    ppermute x1, waiting for transfers between devices: 0.01 us -> 2.63 us  [per_device(): lax.ppermute(edge_rows(edge_pixels, edge_mask), 'group', [(i, (i + 1) % g...]
    all_to_all x2, waiting for transfers between devices: 0.01 us -> 2.61 us  [per_device(): lax.all_to_all(pooled, 'date', split_axis=0, concat_axis=0, tiled=True)]
    all_to_all x2, starting transfers between devices: 15.4 us -> 13.7 us  [per_device(): lax.all_to_all(pooled, 'date', split_axis=0, concat_axis=0, tiled=True)]
  transfers between devices with their start and end apart: 3 -> 3, of which waited for: 0 -> 3; matrix products, arithmetic and copies ran while one was open for 4% -> 2% of each run, Pallas kernels for 49% -> 38%
where the time goes in v4:
time: 95.2 us; the launch traced here: 94.9 us
  Pallas kernels  71.2 us (75%)
  starting transfers between devices  16.1 us (17%)
  waiting for transfers between devices  5.25 us (6%)
  other arithmetic  1.49 us (2%)
    pallas_call x2, Pallas kernels, attend(): pl.pallas_call(functools.partial(attention_kernel, last=last), out_shape=...  34.6 us
    pallas_call x2, Pallas kernels, pool_lots(): pl.pallas_call(functools.partial(pixel_kernel, chunk=chunk), grid=(blocks...  29.4 us
    all_to_all x2, starting transfers between devices, per_device(): lax.all_to_all(pooled, 'date', split_axis=0, concat_axis=0, tiled=True)  13.7 us
    pallas_call x1, Pallas kernels, lay_out(): pl.pallas_call(lay_out_kernel, grid=(blocks,), in_specs=[pl.BlockSpec((ba...  5.35 us
    ppermute x1, waiting for transfers between devices, per_device(): lax.ppermute(edge_rows(edge_pixels, edge_mask), 'group', [(i, (i + 1) % g...  2.63 us
    all_to_all x2, waiting for transfers between devices, per_device(): lax.all_to_all(pooled, 'date', split_axis=0, concat_axis=0, tiled=True)  2.61 us
    ppermute x1, starting transfers between devices, per_device(): lax.ppermute(edge_rows(edge_pixels, edge_mask), 'group', [(i, (i + 1) % g...  2.47 us
  transfers between devices with their start and end apart: 3, of which 3 were waited for; matrix products, arithmetic and copies ran while one was open for 2% of the time, Pallas kernels for 38%

profile of v4, /device:TPU:1, one launch (start us, length us, event | category | flops | bytes accessed | tf_op | source)
XLA Modules:
  0.0 94.9 jit_solution(8203232130615840737)
XLA Ops:
  0.0 1.8 %edge_rows.1 = bf16[14,4,16,128]{3,2,1,0:T(8,128)(2,1)} custom-call(bf16[13,8,16,64]{3,2,1,0:T(8,128)(2,1)} %pix_ref.3, s32[8,16,64]{2,1,0:T(8,128)} %mask_ref.1), custom_call_target="tpu_custom_call" | custom-call | tf_op jit(solution)/shard_map/edge_rows/pallas_call | solution.py:436
  1.8 2.5 %collective-permute-start = (bf16[14,4,16,128]{3,2,1,0:T(8,128)(2,1)}, bf16[14,4,16,128]{3,2,1,0:T(8,128)(2,1)S(1)}, u32[]{:S(2)}, u32[]{:S(2)}) collective-permute-start(bf16[14,4,16,128]{3,2,1,0:T(8,128)(2,1)} %edge_rows.1), channel_id=1, source_target_pairs={{0,32},{32,64},{64,96},{96,128},{128,160},{160,192},{192,224},{224... | collective-permute-start | bytes 688136 | tf_op jit(solution)/shard_map/ppermute | solution.py:452
  4.3 0.8 dynamic-slice_convert_fusion
  5.1 5.3 %lay_out.1 = (bf16[2,4,768,256]{3,2,1,0:T(8,128)(2,1)}, bf16[2,4,768,256]{3,2,1,0:T(8,128)(2,1)}) custom-call(bf16[13,24,16,512]{3,2,1,0:T(8,128)(2,1)} %pix_ref.2, s32[16,512]{1,0:T(8,128)} %cnt_ref.5), custom_call_target="tpu_custom_call" | custom-call | tf_op jit(solution)/shard_map/lay_out/pallas_call | solution.py:252
  10.4 0.0 copy-done.9
  10.4 0.7 select_add_fusion.code_ref
  11.2 2.6 %collective-permute-done.edge_ref = bf16[14,4,16,128]{3,2,1,0:T(8,128)(2,1)S(1)} collective-permute-done((bf16[14,4,16,128]{3,2,1,0:T(8,128)(2,1)}, bf16[14,4,16,128]{3,2,1,0:T(8,128)(2,1)S(1)}, u32[]{:S(2)}, u32[]{:S(2)}) %collective-permute-start) | collective-permute-done | bytes 229408 | tf_op jit(solution)/shard_map/ppermute | solution.py:452
  13.8 0.7 copy-done.8
  14.5 14.6 %pixel_pool_0.1 = bf16[32,8,16,128]{3,2,1,0:T(8,128)(2,1)} custom-call(bf16[2,4,768,256]{3,2,1,0:T(8,128)(2,1)} %get-tuple-element.8.xt_ref, s32[16,512]{1,0:T(8,128)} %cnt_ref.5, bf16[14,4,16,128]{3,2,1,0:T(8,128)(2,1)} %copy-done.8, s32[1,64]{1,0:T(1,128)} %bitcast.15, bf16[13,32]{1,0:T(8,128)(2,1)} %bitcast.13, f32[1,32]{1,0:T(1,128)} %bitcast.17, ...), custom_call_target="tpu_custom_call" | custom-call | tf_op jit(solution)/shard_map/pixel_pool_0/pallas_call | solution.py:274
  29.1 8.3 %all-to-all-start.1 = ((bf16[32,8,16,128]{3,2,1,0:T(8,128)(2,1)}), bf16[32,8,16,128]{3,2,1,0:T(8,128)(2,1)S(1)}, u32[]{:S(2)}, u32[]{:S(2)}) async-start(bf16[32,8,16,128]{3,2,1,0:T(8,128)(2,1)} %pixel_pool_0.1), calls=%async_computation.1 | async-start | bytes 2097152 | tf_op jit(solution)/shard_map/all_to_all | solution.py:462
  37.4 0.0 copy-start
  37.5 0.0 copy-start.1
  37.5 0.0 copy-start.2
  37.5 0.0 copy-start.3
  37.5 0.0 copy-start.4
  37.5 0.0 copy-start.5
  37.5 0.0 copy-start.6
  37.5 0.0 copy-start.7
  37.5 14.7 %pixel_pool_1.1 = bf16[32,8,16,128]{3,2,1,0:T(8,128)(2,1)} custom-call(bf16[2,4,768,256]{3,2,1,0:T(8,128)(2,1)} %get-tuple-element.7.xt_ref, s32[16,512]{1,0:T(8,128)} %cnt_ref.5, bf16[14,4,16,128]{3,2,1,0:T(8,128)(2,1)} %copy-done.8, s32[1,64]{1,0:T(1,128)} %bitcast.16, bf16[13,32]{1,0:T(8,128)(2,1)} %bitcast.14, f32[1,32]{1,0:T(1,128)} %bitcast.18, ...), custom_call_target="tpu_custom_call" | custom-call | tf_op jit(solution)/shard_map/pixel_pool_1/pallas_call | solution.py:274
  52.3 2.1 %all-to-all-done.1.e_ref = bf16[32,8,16,128]{3,2,1,0:T(8,128)(2,1)S(1)} async-done(((bf16[32,8,16,128]{3,2,1,0:T(8,128)(2,1)}), bf16[32,8,16,128]{3,2,1,0:T(8,128)(2,1)S(1)}, u32[]{:S(2)}, u32[]{:S(2)}) %all-to-all-start.1) | async-done | bytes 1048608 | tf_op jit(solution)/shard_map/all_to_all | solution.py:462
  54.3 5.3 %all-to-all-start = ((bf16[32,8,16,128]{3,2,1,0:T(8,128)(2,1)}), bf16[32,8,16,128]{3,2,1,0:T(8,128)(2,1)S(1)}, u32[]{:S(2)}, u32[]{:S(2)}) async-start(bf16[32,8,16,128]{3,2,1,0:T(8,128)(2,1)} %pixel_pool_1.1), calls=%async_computation | async-start | bytes 2097152 | tf_op jit(solution)/shard_map/all_to_all | solution.py:462
  59.8 16.3 %attend_first.1.rest_0_ = bf16[8,32,16,128]{3,2,1,0:T(8,128)(2,1)S(1)} custom-call(bf16[32,8,16,128]{3,2,1,0:T(8,128)(2,1)S(1)} %all-to-all-done.1.e_ref, f32[1,128]{1,0:T(1,128)S(1)} %bitcast.7, bf16[128,128]{1,0:T(8,128)(2,1)S(1)} %copy-done.2, bf16[128,128]{1,0:T(8,128)(2,1)S(1)} %copy-done.3, bf16[128,128]{1,0:T(8,128)(2,1)S(1)} %copy-done.4, ...), custom_call_target="tpu_custom_call" | custom-call | tf_op jit(solution)/shard_map/attend_first/pallas_call | solution.py:407
  76.0 0.5 all-to-all-done.e_ref
  76.6 18.3 %attend_last.1 = bf16[512,16,128]{2,1,0:T(8,128)(2,1)} custom-call(bf16[32,8,16,128]{3,2,1,0:T(8,128)(2,1)S(1)} %all-to-all-done.e_ref, f32[1,128]{1,0:T(1,128)S(1)} %bitcast.8, bf16[128,128]{1,0:T(8,128)(2,1)S(1)} %copy-done.2, bf16[128,128]{1,0:T(8,128)(2,1)S(1)} %copy-done.3, bf16[128,128]{1,0:T(8,128)(2,1)S(1)} %copy-done.4, ...), custom_call_target="tpu_custom_call" | custom-call | tf_op jit(solution)/shard_map/attend_last/pallas_call | solution.py:407
  (13 shorter events, 0.0 us)
Async XLA Ops:
  0.0 10.4 %copy-start.9 = (f32[128]{0:T(128)S(1)}, f32[128]{0:T(128)}, u32[]{:S(2)}) copy-start(f32[128]{0:T(128)} %param.31) | copy-start | bytes 1540
  1.8 11.9 %collective-permute-start = (bf16[14,4,16,128]{3,2,1,0:T(8,128)(2,1)}, bf16[14,4,16,128]{3,2,1,0:T(8,128)(2,1)S(1)}, u32[]{:S(2)}, u32[]{:S(2)}) collective-permute-start(bf16[14,4,16,128]{3,2,1,0:T(8,128)(2,1)} %edge_rows.1), channel_id=1, source_target_pairs={{0,32},{32,64},{64,96},{96,128},{128,160},{160,192},{192,224},{224... | collective-permute-start | bytes 688136 | tf_op jit(solution)/shard_map/ppermute | solution.py:452
  13.8 0.7 copy-start.8
  29.1 25.2 %all-to-all-start.1 = ((bf16[32,8,16,128]{3,2,1,0:T(8,128)(2,1)}), bf16[32,8,16,128]{3,2,1,0:T(8,128)(2,1)S(1)}, u32[]{:S(2)}, u32[]{:S(2)}) async-start(bf16[32,8,16,128]{3,2,1,0:T(8,128)(2,1)} %pixel_pool_0.1), calls=%async_computation.1 | async-start | bytes 2097152 | tf_op jit(solution)/shard_map/all_to_all | solution.py:462
  37.4 22.2 %copy-start = (bf16[128,512]{1,0:T(8,128)(2,1)S(1)}, bf16[128,512]{1,0:T(8,128)(2,1)}, u32[]{:S(2)}) copy-start(bf16[128,512]{1,0:T(8,128)(2,1)} %up_ref.3) | copy-start | bytes 393220
  37.5 22.2 %copy-start.1 = (bf16[512,128]{1,0:T(8,128)(2,1)S(1)}, bf16[512,128]{1,0:T(8,128)(2,1)}, u32[]{:S(2)}) copy-start(bf16[512,128]{1,0:T(8,128)(2,1)} %down_ref.3) | copy-start | bytes 393220
  37.5 22.2 %copy-start.2 = (bf16[128,128]{1,0:T(8,128)(2,1)S(1)}, bf16[128,128]{1,0:T(8,128)(2,1)}, u32[]{:S(2)}) copy-start(bf16[128,128]{1,0:T(8,128)(2,1)} %wq_ref.3) | copy-start | bytes 98308
  37.5 22.2 %copy-start.3 = (bf16[128,128]{1,0:T(8,128)(2,1)S(1)}, bf16[128,128]{1,0:T(8,128)(2,1)}, u32[]{:S(2)}) copy-start(bf16[128,128]{1,0:T(8,128)(2,1)} %wk_ref.3) | copy-start | bytes 98308
  37.5 22.2 %copy-start.4 = (bf16[128,128]{1,0:T(8,128)(2,1)S(1)}, bf16[128,128]{1,0:T(8,128)(2,1)}, u32[]{:S(2)}) copy-start(bf16[128,128]{1,0:T(8,128)(2,1)} %wv_ref.3) | copy-start | bytes 98308
  37.5 22.2 %copy-start.5 = (bf16[128,128]{1,0:T(8,128)(2,1)S(1)}, bf16[128,128]{1,0:T(8,128)(2,1)}, u32[]{:S(2)}) copy-start(bf16[128,128]{1,0:T(8,128)(2,1)} %wo_ref.3) | copy-start | bytes 98308
  37.5 22.2 %copy-start.6 = (f32[128]{0:T(128)S(1)}, f32[128]{0:T(128)}, u32[]{:S(2)}) copy-start(f32[128]{0:T(128)} %param.32) | copy-start | bytes 1540
  37.5 22.2 %copy-start.7 = (f32[128]{0:T(128)S(1)}, f32[128]{0:T(128)}, u32[]{:S(2)}) copy-start(f32[128]{0:T(128)} %param.37) | copy-start | bytes 1540
  54.3 22.2 %all-to-all-start = ((bf16[32,8,16,128]{3,2,1,0:T(8,128)(2,1)}), bf16[32,8,16,128]{3,2,1,0:T(8,128)(2,1)S(1)}, u32[]{:S(2)}, u32[]{:S(2)}) async-start(bf16[32,8,16,128]{3,2,1,0:T(8,128)(2,1)} %pixel_pool_1.1), calls=%async_computation | async-start | bytes 2097152 | tf_op jit(solution)/shard_map/all_to_all | solution.py:462

commit v5 on v4

--- a/solution.py
+++ b/solution.py
@@ -295,7 +295,7 @@
             pltpu.VMEM((dates, LANES, LANES), BF16),
             pltpu.VMEM((256, 256), BF16),
         ],
-        compiler_params=pltpu.CompilerParams(vmem_limit_bytes=58 << 20),
+        compiler_params=pltpu.CompilerParams(vmem_limit_bytes=52 << 20),
         name=f"pixel_pool_{chunk}",
     )(laid, counts, *fixed)
 
@@ -322,7 +322,7 @@
     total = peers * dates
     head = width // HEADS
     together = q_ref.shape[0]
-    tall = 256
+    tall = 512
     scale = math.log2(math.e) / math.sqrt(head)
 
     def rows_of(lot):

time: 95.2 us -> 94.3 us (level)
  transfers between devices with their start and end apart: 3 -> 3, of which waited for: 3 -> 3; matrix products, arithmetic and copies ran while one was open for 2% -> 1% of each run, Pallas kernels for 38% -> 38%
where the time goes in v5:
time: 94.3 us; the launch traced here: 93.9 us
  Pallas kernels  70.5 us (75%)
  starting transfers between devices  16 us (17%)
  waiting for transfers between devices  6.17 us (7%)
    pallas_call x2, Pallas kernels, attend(): pl.pallas_call(functools.partial(attention_kernel, last=last), out_shape=...  34.2 us
    pallas_call x2, Pallas kernels, pool_lots(): pl.pallas_call(functools.partial(pixel_kernel, chunk=chunk), grid=(blocks...  29.1 us
    all_to_all x2, starting transfers between devices, per_device(): lax.all_to_all(pooled, 'date', split_axis=0, concat_axis=0, tiled=True)  13.5 us
    pallas_call x1, Pallas kernels, lay_out(): pl.pallas_call(lay_out_kernel, grid=(blocks,), in_specs=[pl.BlockSpec((ba...  5.33 us
    ppermute x1, waiting for transfers between devices, per_device(): lax.ppermute(edge_rows(edge_pixels, edge_mask), 'group', [(i, (i + 1) % g...  3.24 us
    all_to_all x2, waiting for transfers between devices, per_device(): lax.all_to_all(pooled, 'date', split_axis=0, concat_axis=0, tiled=True)  2.92 us
    ppermute x1, starting transfers between devices, per_device(): lax.ppermute(edge_rows(edge_pixels, edge_mask), 'group', [(i, (i + 1) % g...  2.47 us
    pallas_call x1, Pallas kernels, edge_rows(): pl.pallas_call(edge_kernel, out_shape=jax.ShapeDtypeStruct((bands + 1, sl...  1.91 us
  transfers between devices with their start and end apart: 3, of which 3 were waited for; matrix products, arithmetic and copies ran while one was open for 1% of the time, Pallas kernels for 38%

profile of v5, /device:TPU:1, one launch (start us, length us, event | category | flops | bytes accessed | tf_op | source)
XLA Modules:
  0.0 93.9 jit_solution(1869554478745997067)
XLA Ops:
  0.0 0.0 copy-start.12
  0.0 0.0 copy-start.8
  0.1 1.9 %edge_rows.1 = bf16[14,4,16,128]{3,2,1,0:T(8,128)(2,1)} custom-call(bf16[13,8,16,64]{3,2,1,0:T(8,128)(2,1)} %pix_ref.3, s32[8,16,64]{2,1,0:T(8,128)} %mask_ref.1), custom_call_target="tpu_custom_call" | custom-call | tf_op jit(solution)/shard_map/edge_rows/pallas_call | solution.py:436
  2.0 2.5 %collective-permute-start = (bf16[14,4,16,128]{3,2,1,0:T(8,128)(2,1)}, bf16[14,4,16,128]{3,2,1,0:T(8,128)(2,1)S(1)}, u32[]{:S(2)}, u32[]{:S(2)}) collective-permute-start(bf16[14,4,16,128]{3,2,1,0:T(8,128)(2,1)} %edge_rows.1), channel_id=1, source_target_pairs={{0,32},{32,64},{64,96},{96,128},{128,160},{160,192},{192,224},{224... | collective-permute-start | bytes 688136 | tf_op jit(solution)/shard_map/ppermute | solution.py:452
  4.5 0.8 dynamic-slice_convert_fusion
  5.2 5.3 %lay_out.1 = (bf16[2,4,768,256]{3,2,1,0:T(8,128)(2,1)}, bf16[2,4,768,256]{3,2,1,0:T(8,128)(2,1)}) custom-call(bf16[13,24,16,512]{3,2,1,0:T(8,128)(2,1)} %pix_ref.2, s32[16,512]{1,0:T(8,128)} %cnt_ref.5), custom_call_target="tpu_custom_call" | custom-call | tf_op jit(solution)/shard_map/lay_out/pallas_call | solution.py:252
  10.5 0.1 select_add_fusion.code_ref
  10.7 3.2 %collective-permute-done.edge_ref = bf16[14,4,16,128]{3,2,1,0:T(8,128)(2,1)S(1)} collective-permute-done((bf16[14,4,16,128]{3,2,1,0:T(8,128)(2,1)}, bf16[14,4,16,128]{3,2,1,0:T(8,128)(2,1)S(1)}, u32[]{:S(2)}, u32[]{:S(2)}) %collective-permute-start) | collective-permute-done | bytes 229408 | tf_op jit(solution)/shard_map/ppermute | solution.py:452
  14.0 14.5 %pixel_pool_0.1 = bf16[32,8,16,128]{3,2,1,0:T(8,128)(2,1)} custom-call(bf16[2,4,768,256]{3,2,1,0:T(8,128)(2,1)} %get-tuple-element.8.xt_ref, s32[16,512]{1,0:T(8,128)S(1)} %copy-done.2, bf16[14,4,16,128]{3,2,1,0:T(8,128)(2,1)S(1)} %collective-permute-done.edge_ref, s32[1,64]{1,0:T(1,128)S(1)} %bitcast.11, bf16[13,32]{1,0:T(8,128)(2,1)S(1)} %bitcast.9, ...), custom_call_target="tpu_custom_call" | custom-call | tf_op jit(solution)/shard_map/pixel_pool_0/pallas_call | solution.py:274
  28.5 8.3 %all-to-all-start.1 = ((bf16[32,8,16,128]{3,2,1,0:T(8,128)(2,1)}), bf16[32,8,16,128]{3,2,1,0:T(8,128)(2,1)S(1)}, u32[]{:S(2)}, u32[]{:S(2)}) async-start(bf16[32,8,16,128]{3,2,1,0:T(8,128)(2,1)} %pixel_pool_0.1), calls=%async_computation.1 | async-start | bytes 2097152 | tf_op jit(solution)/shard_map/all_to_all | solution.py:462
  36.8 0.0 copy-start
  36.8 0.0 copy-start.1
  36.8 0.0 copy-start.4
  36.8 0.0 copy-start.5
  36.8 0.0 copy-start.6
  36.9 0.0 copy-start.7
  36.9 0.0 copy-start.13
  36.9 0.0 copy-start.14
  36.9 14.6 %pixel_pool_1.1 = bf16[32,8,16,128]{3,2,1,0:T(8,128)(2,1)} custom-call(bf16[2,4,768,256]{3,2,1,0:T(8,128)(2,1)} %get-tuple-element.7.xt_ref, s32[16,512]{1,0:T(8,128)S(1)} %copy-done.2, bf16[14,4,16,128]{3,2,1,0:T(8,128)(2,1)S(1)} %collective-permute-done.edge_ref, s32[1,64]{1,0:T(1,128)S(1)} %bitcast.12, bf16[13,32]{1,0:T(8,128)(2,1)S(1)} %bitcast.10, ...), custom_call_target="tpu_custom_call" | custom-call | tf_op jit(solution)/shard_map/pixel_pool_1/pallas_call | solution.py:274
  51.5 2.2 %all-to-all-done.1.e_ref = bf16[32,8,16,128]{3,2,1,0:T(8,128)(2,1)S(1)} async-done(((bf16[32,8,16,128]{3,2,1,0:T(8,128)(2,1)}), bf16[32,8,16,128]{3,2,1,0:T(8,128)(2,1)S(1)}, u32[]{:S(2)}, u32[]{:S(2)}) %all-to-all-start.1) | async-done | bytes 1048608 | tf_op jit(solution)/shard_map/all_to_all | solution.py:462
  53.7 5.2 %all-to-all-start = ((bf16[32,8,16,128]{3,2,1,0:T(8,128)(2,1)}), bf16[32,8,16,128]{3,2,1,0:T(8,128)(2,1)S(1)}, u32[]{:S(2)}, u32[]{:S(2)}) async-start(bf16[32,8,16,128]{3,2,1,0:T(8,128)(2,1)} %pixel_pool_1.1), calls=%async_computation | async-start | bytes 2097152 | tf_op jit(solution)/shard_map/all_to_all | solution.py:462
  59.0 16.1 %attend_first.1.rest_0_ = bf16[8,32,16,128]{3,2,1,0:T(8,128)(2,1)S(1)} custom-call(bf16[32,8,16,128]{3,2,1,0:T(8,128)(2,1)S(1)} %all-to-all-done.1.e_ref, f32[1,128]{1,0:T(1,128)S(1)} %bitcast.17, bf16[128,128]{1,0:T(8,128)(2,1)S(1)} %copy-done.4, bf16[128,128]{1,0:T(8,128)(2,1)S(1)} %copy-done.5, bf16[128,128]{1,0:T(8,128)(2,1)S(1)} %copy-done.6, ...), custom_call_target="tpu_custom_call" | custom-call | tf_op jit(solution)/shard_map/attend_first/pallas_call | solution.py:407
  75.1 0.8 all-to-all-done.e_ref
  75.8 18.1 %attend_last.1 = bf16[512,16,128]{2,1,0:T(8,128)(2,1)} custom-call(bf16[32,8,16,128]{3,2,1,0:T(8,128)(2,1)S(1)} %all-to-all-done.e_ref, f32[1,128]{1,0:T(1,128)S(1)} %bitcast.18, bf16[128,128]{1,0:T(8,128)(2,1)S(1)} %copy-done.4, bf16[128,128]{1,0:T(8,128)(2,1)S(1)} %copy-done.5, bf16[128,128]{1,0:T(8,128)(2,1)S(1)} %copy-done.6, ...), custom_call_target="tpu_custom_call" | custom-call | tf_op jit(solution)/shard_map/attend_last/pallas_call | solution.py:407
  (25 shorter events, 0.1 us)
Async XLA Ops:
  0.0 13.9 %copy-start.2 = (s32[16,512]{1,0:T(8,128)S(1)}, s32[16,512]{1,0:T(8,128)}, u32[]{:S(2)}) copy-start(s32[16,512]{1,0:T(8,128)} %cnt_ref.5) | copy-start | bytes 98308
  0.0 10.5 %copy-start.15 = (f32[128]{0:T(128)S(1)}, f32[128]{0:T(128)}, u32[]{:S(2)}) copy-start(f32[128]{0:T(128)} %param.31) | copy-start | bytes 1540
  0.0 13.9 %copy-start.3 = (bf16[256,128]{1,0:T(8,128)(2,1)S(1)}, bf16[256,128]{1,0:T(8,128)(2,1)}, u32[]{:S(2)}) copy-start(bf16[256,128]{1,0:T(8,128)(2,1)} %wp_ref.3) | copy-start | bytes 196612
  0.0 13.9 %copy-start.12 = (f32[128]{0:T(128)S(1)}, f32[128]{0:T(128)}, u32[]{:S(2)}) copy-start(f32[128]{0:T(128)} %param.29) | copy-start | bytes 1540
  0.0 13.9 %copy-start.8 = (bf16[128,32]{0,1:T(8,128)(2,1)S(1)}, bf16[128,32]{0,1:T(8,128)(2,1)}, u32[]{:S(2)}) copy-start(bf16[128,32]{0,1:T(8,128)(2,1)} %param.28) | copy-start | bytes 24580
  0.0 13.9 %copy-start.11 = (f32[32]{0:T(128)S(1)}, f32[32]{0:T(128)}, u32[]{:S(2)}) copy-start(f32[32]{0:T(128)} %param.27) | copy-start | bytes 388
  0.0 13.9 %copy-start.9 = (bf16[32,13]{0,1:T(8,128)(2,1)S(1)}, bf16[32,13]{0,1:T(8,128)(2,1)}, u32[]{:S(2)}) copy-start(bf16[32,13]{0,1:T(8,128)(2,1)} %param.26) | copy-start | bytes 2500
  0.0 13.9 %copy-start.10 = (s32[64]{0:T(128)S(1)}, s32[64]{0:T(128)}, u32[]{:S(2)}) copy-start(s32[64]{0:T(128)} %param.24) | copy-start | bytes 772
  2.0 11.9 %collective-permute-start = (bf16[14,4,16,128]{3,2,1,0:T(8,128)(2,1)}, bf16[14,4,16,128]{3,2,1,0:T(8,128)(2,1)S(1)}, u32[]{:S(2)}, u32[]{:S(2)}) collective-permute-start(bf16[14,4,16,128]{3,2,1,0:T(8,128)(2,1)} %edge_rows.1), channel_id=1, source_target_pairs={{0,32},{32,64},{64,96},{96,128},{128,160},{160,192},{192,224},{224... | collective-permute-start | bytes 688136 | tf_op jit(solution)/shard_map/ppermute | solution.py:452
  28.5 25.2 %all-to-all-start.1 = ((bf16[32,8,16,128]{3,2,1,0:T(8,128)(2,1)}), bf16[32,8,16,128]{3,2,1,0:T(8,128)(2,1)S(1)}, u32[]{:S(2)}, u32[]{:S(2)}) async-start(bf16[32,8,16,128]{3,2,1,0:T(8,128)(2,1)} %pixel_pool_0.1), calls=%async_computation.1 | async-start | bytes 2097152 | tf_op jit(solution)/shard_map/all_to_all | solution.py:462
  36.8 22.1 %copy-start = (bf16[128,512]{1,0:T(8,128)(2,1)S(1)}, bf16[128,512]{1,0:T(8,128)(2,1)}, u32[]{:S(2)}) copy-start(bf16[128,512]{1,0:T(8,128)(2,1)} %up_ref.3) | copy-start | bytes 393220
  36.8 22.1 %copy-start.1 = (bf16[512,128]{1,0:T(8,128)(2,1)S(1)}, bf16[512,128]{1,0:T(8,128)(2,1)}, u32[]{:S(2)}) copy-start(bf16[512,128]{1,0:T(8,128)(2,1)} %down_ref.3) | copy-start | bytes 393220
  36.8 22.1 %copy-start.4 = (bf16[128,128]{1,0:T(8,128)(2,1)S(1)}, bf16[128,128]{1,0:T(8,128)(2,1)}, u32[]{:S(2)}) copy-start(bf16[128,128]{1,0:T(8,128)(2,1)} %wq_ref.3) | copy-start | bytes 98308
  36.8 22.1 %copy-start.5 = (bf16[128,128]{1,0:T(8,128)(2,1)S(1)}, bf16[128,128]{1,0:T(8,128)(2,1)}, u32[]{:S(2)}) copy-start(bf16[128,128]{1,0:T(8,128)(2,1)} %wk_ref.3) | copy-start | bytes 98308
  36.8 22.1 %copy-start.6 = (bf16[128,128]{1,0:T(8,128)(2,1)S(1)}, bf16[128,128]{1,0:T(8,128)(2,1)}, u32[]{:S(2)}) copy-start(bf16[128,128]{1,0:T(8,128)(2,1)} %wv_ref.3) | copy-start | bytes 98308
  36.9 22.1 %copy-start.7 = (bf16[128,128]{1,0:T(8,128)(2,1)S(1)}, bf16[128,128]{1,0:T(8,128)(2,1)}, u32[]{:S(2)}) copy-start(bf16[128,128]{1,0:T(8,128)(2,1)} %wo_ref.3) | copy-start | bytes 98308
  36.9 22.1 %copy-start.13 = (f32[128]{0:T(128)S(1)}, f32[128]{0:T(128)}, u32[]{:S(2)}) copy-start(f32[128]{0:T(128)} %param.32) | copy-start | bytes 1540
  36.9 22.1 %copy-start.14 = (f32[128]{0:T(128)S(1)}, f32[128]{0:T(128)}, u32[]{:S(2)}) copy-start(f32[128]{0:T(128)} %param.37) | copy-start | bytes 1540
  53.7 22.1 %all-to-all-start = ((bf16[32,8,16,128]{3,2,1,0:T(8,128)(2,1)}), bf16[32,8,16,128]{3,2,1,0:T(8,128)(2,1)S(1)}, u32[]{:S(2)}, u32[]{:S(2)}) async-start(bf16[32,8,16,128]{3,2,1,0:T(8,128)(2,1)} %pixel_pool_1.1), calls=%async_computation | async-start | bytes 2097152 | tf_op jit(solution)/shard_map/all_to_all | solution.py:462
